TPU v7x, 768 devices: a whole 4x8x12 slice. The times are simulated.
768 devices in a mesh: dp: 64 (over z_hi, y, core), chan: 12 (over x, z_lo).
Axes of the slice: x: 4, y: 8, z: 12 (z_hi: 4, z_lo: 3; z = z_hi * 3 + z_lo), core: 2. Of those that a mesh axis runs over, the one named last changes fastest.
Arguments:
- hidden: bfloat16 [128, 14, 14, 3072], P('dp', None, None, 'chan'), may hold values from -6 to 6
- conv_weight: bfloat16 [3, 3, 64, 3072], P(None, None, None, 'chan'), may hold values from -0.25 to 0.25
- se_down: bfloat16 [3072, 1024], P('chan'), may hold values from -0.875 to 0.875
- se_up: bfloat16 [1024, 3072], P(None, 'chan'), may hold values from -0.75 to 0.75
- proj_weight: bfloat16 [3072, 3072], P('chan'), may hold values from -0.109375 to 0.109375
- grad_out: bfloat16 [128, 14, 14, 3072], P('dp', None, None, 'chan'), may hold values from -16 to 16
Outputs:
- projected: bfloat16 [128, 14, 14, 3072], P('dp', None, None, 'chan')
- grad_hidden: bfloat16 [128, 14, 14, 3072], P('dp', None, None, 'chan')
- grad_proj: float32 [3072, 3072], P('chan', 'dp')
All inputs are finite; a program needn't handle non-finite values.
Results may differ from a plain program's by a relative error of at most 0.024.
Values may be sent and summed in bfloat16 or wider, within the bound.
A program may use at most 64 MiB of HBM per device.

v0:
```python
import jax
import jax.numpy as jnp
from jax import lax
from jax.sharding import PartitionSpec as P


def grouped(inputs, kernel):
    return lax.conv_general_dilated(
        inputs,
        kernel,
        (1, 1),
        "SAME",
        dimension_numbers=("NHWC", "HWIO", "NHWC"),
        feature_group_count=kernel.shape[3] // kernel.shape[2],
        preferred_element_type=jnp.float32,
    )


def turned(kernel):
    size_in = kernel.shape[2]
    group_count = kernel.shape[3] // size_in
    split = kernel.reshape(3, 3, size_in, group_count, size_in)
    return jnp.transpose(split, (0, 1, 4, 3, 2))[::-1, ::-1].reshape(kernel.shape)


def silu_grad(values):
    logistic = jax.nn.sigmoid(values)
    return logistic * (1.0 + values * (1.0 - logistic))


def on_device(hidden, conv_weight, se_down, se_up, proj_weight, grad_out):
    highest = lax.Precision.HIGHEST
    local_ch = hidden.shape[3]
    cells = hidden.shape[1] * hidden.shape[2]
    convolved = grouped(hidden, conv_weight)
    activated = jax.nn.silu(convolved).astype(jnp.bfloat16)
    act_float = activated.astype(jnp.float32)
    squeezed = jnp.mean(act_float, axis=(1, 2))
    excite_pre = lax.psum(jnp.dot(squeezed, se_down.astype(jnp.float32), precision=highest), "chan")
    gating = jax.nn.sigmoid(
        jnp.dot(jax.nn.silu(excite_pre), se_up.astype(jnp.float32), precision=highest)
    )
    scaled = (act_float * gating[:, None, None, :]).astype(jnp.bfloat16)
    act_rows = scaled.reshape(-1, local_ch)
    weight_cols = proj_weight
    summed = lax.psum_scatter(
        lax.dot_general(
            weight_cols, act_rows, (((0,), (1,)), ((), ())), preferred_element_type=jnp.float32
        ).astype(jnp.bfloat16),
        "chan",
        scatter_dimension=0,
        tiled=True,
    ).astype(jnp.float32)
    out_rows = summed.T
    projected = out_rows.astype(jnp.bfloat16).reshape(hidden.shape)
    shard_piece = lax.all_gather(grad_out, "chan", axis=3, tiled=True)
    width_in = shard_piece.shape[3]
    piece_rows = shard_piece.reshape(-1, width_in)
    weight_cols = proj_weight
    dv_next = lax.dot_general(
        piece_rows, weight_cols, (((1,), (1,)), ((), ())), preferred_element_type=jnp.float32
    )
    dw_block = lax.dot_general(
        act_rows, piece_rows, (((0,), (0,)), ((), ())), preferred_element_type=jnp.float32
    )
    grad_proj = lax.psum_scatter(dw_block, "dp", scatter_dimension=1, tiled=True)
    scaled_grad = dv_next.reshape(hidden.shape)
    gate_grad = jnp.sum(scaled_grad * act_float, axis=(1, 2))
    pre_grad = gate_grad * gating * (1.0 - gating)
    excite_sum = lax.psum(jnp.dot(pre_grad, se_up.astype(jnp.float32).T, precision=highest), "chan")
    excite_grad = excite_sum * silu_grad(excite_pre)
    squeeze_grad = jnp.dot(excite_grad, se_down.astype(jnp.float32).T, precision=highest)
    act_grad = scaled_grad * gating[:, None, None, :] + squeeze_grad[:, None, None, :] / cells
    conv_grad = (act_grad * silu_grad(convolved)).astype(jnp.bfloat16)
    grad_hidden = grouped(conv_grad, turned(conv_weight)).astype(jnp.bfloat16)
    return (projected, grad_hidden, grad_proj)


def solution(mesh):
    in_specs = (
        P("dp", None, None, "chan"),
        P(None, None, None, "chan"),
        P("chan", None),
        P(None, "chan"),
        P("chan", None),
        P("dp", None, None, "chan"),
    )
    out_specs = (P("dp", None, None, "chan"), P("dp", None, None, "chan"), P("chan", "dp"))
    return jax.shard_map(
        on_device, mesh=mesh, in_specs=in_specs, out_specs=out_specs, check_vma=False
    )
```

profile of v0, /device:TPU:1, one launch (start us, length us, event | category | flops | bytes accessed | tf_op | source)
XLA Modules:
  0.0 363.9 jit_solution(7406947657636631751)
XLA Ops:
  7.2 0.0 copy-start
  7.2 0.0 all-gather.2.cloned.1.call-start
  7.2 1.8 copy.59
  9.0 0.0 all-gather.2.cloned.1.call-update
  9.0 0.0 reduce-scatter.3.cloned.1.call-start
  9.1 1.3 shard_map.90
  10.4 0.0 copy-start.5
  10.4 2.2 shard_map.89
  12.6 0.0 copy-start.3
  12.6 0.0 copy-start.1
  12.6 4.4 %convert_reduce_fusion = (f32[2,4,64]{2,0,1:T(2,128)S(1)}, f32[2,14,14,4,64]{4,0,3,2,1:T(2,128)}) fusion(bf16[3,3,64,4,64]{4,3,2,1,0:T(4,128)(2,1)S(1)} %shard_map.90, bf16[2,14,14,4,64]{4,3,0,2,1:T(4,128)(2,1)} %shard_map.89), kind=kOutput, calls=%fused_computation.12 | convolution fusion | flops 105559552 | bytes 899072 | tf_op jit(solution)/shard_map/conv_general_dilated | solution.py:8
  17.0 0.0 copy-done.5
  17.0 0.1 div.37
  17.1 0.0 copy-done.3
  17.1 0.3 fusion.32
  17.4 29.1 %psum.14 = f32[2,1024]{1,0:T(2,128)S(1)} all-reduce(f32[2,1024]{1,0:T(2,128)S(1)} %fusion.32), channel_id=1, replica_groups=mesh['dp'=64,'chan'=12] {'chan'}, use_global_device_ids=true, to_apply=%region_1.2 | all-reduce | flops 2048 | bytes 16384 | tf_op jit(solution)/shard_map/psum | solution.py:39
  46.5 0.0 copy-done.1
  46.5 0.3 fusion.5
  46.9 0.1 mul.64
  46.9 1.4 copy.57
  48.3 0.5 conv_general_dilated.11
  48.8 0.0 copy-done
  48.8 2.3 fusion
  51.0 0.0 reduce-scatter.3.cloned.1.call-update
  51.1 0.0 reduce-scatter.5.cloned.1.call-start
  51.1 0.4 reshape.36
  51.6 45.9 %all-gather.2.cloned.1.call-done = bf16[2,14,14,3072]{3,2,1,0:T(8,128)(2,1)} async-done(((bf16[2,14,14,256]{3,2,1,0:T(8,128)(2,1)}), bf16[2,14,14,3072]{3,2,1,0:T(8,128)(2,1)}) %all-gather.2.cloned.1.call-update) | async-done | bytes 2408464 | tf_op jit(solution)/shard_map/all_gather | solution.py:56
  97.5 4.8 %convolution_bitcast_fusion = f32[256,3072]{0,1:T(8,128)} fusion(bf16[2,14,14,3072]{3,2,1,0:T(8,128)(2,1)} %all-gather.2.cloned.1.call-done, f32[2,256]{1,0:T(2,128)S(1)} %fusion.5, f32[2,14,14,256]{3,2,1,0:T(8,128)S(1)} %reshape.36), kind=kOutput, calls=%fused_computation.1 | convolution fusion | flops 617365504 | bytes 5957632 | tf_op jit(solution)/shard_map/dot_general | solution.py:63
  102.3 0.0 reduce-scatter.5.cloned.1.call-update
  102.3 0.0 copy-start.2
  102.3 0.0 copy-start.4
  102.3 3.6 fusion.10
  106.0 0.0 copy-start.6
  106.0 0.0 copy-done.2
  106.0 0.5 fusion.24
  106.5 23.9 %psum.15 = f32[2,1024]{1,0:T(2,128)S(1)} all-reduce(f32[2,1024]{1,0:T(2,128)S(1)} %fusion.24), channel_id=1, replica_groups=mesh['dp'=64,'chan'=12] {'chan'}, use_global_device_ids=true, to_apply=%region_4.5 | all-reduce | flops 2048 | bytes 16384 | tf_op jit(solution)/shard_map/psum | solution.py:70
  130.4 0.0 copy-done.4
  130.4 0.5 convolution_multiply_fusion
  130.9 1.2 multiply_convert_fusion
  132.1 0.2 reshape.35
  132.3 0.0 copy-done.6
  132.3 4.2 %convolution_convert_fusion.1 = bf16[2,14,14,4,64]{4,0,3,2,1:T(2,128)(2,1)S(1)} fusion(bf16[3,3,64,4,64]{4,3,2,1,0:T(4,128)(2,1)S(1)} %copy-done.6, bf16[2,14,14,4,64]{4,3,2,1,0:T(4,128)(2,1)S(1)} %reshape.35), kind=kOutput, calls=%fused_computation.5 | convolution fusion | flops 104957952 | bytes 696320 | tf_op jit(solution)/shard_map/conv_general_dilated | solution.py:8
  136.6 0.1 copy.67
  136.7 1.0 convert_element_type.63
  137.7 40.3 %reduce-scatter.3.cloned.1.call-done = bf16[256,392]{0,1:T(8,128)(2,1)} async-done(((bf16[3072,392]{0,1:T(8,128)(2,1)}), bf16[256,392]{0,1:T(8,128)(2,1)}) %reduce-scatter.3.cloned.1.call-update) | async-done | bytes 200720 | tf_op jit(solution)/shard_map/reduce_scatter | solution.py:46
  178.0 1.0 reshape.32
  179.0 0.9 copy.68
  179.9 177.5 %reduce-scatter.5.cloned.1.call-done = f32[256,48]{0,1:T(8,128)} async-done(((f32[256,3072]{0,1:T(8,128)}), f32[256,48]{0,1:T(8,128)}) %reduce-scatter.5.cloned.1.call-update) | async-done | bytes 49168 | tf_op jit(solution)/shard_map/reduce_scatter | solution.py:66
  (2 shorter events, 0.1 us)
Async XLA Ops:
  7.2 41.6 %copy-start = (bf16[256,3072]{1,0:T(8,128)(2,1)S(1)}, bf16[256,3072]{1,0:T(8,128)(2,1)}, u32[]{:S(2)}) copy-start(bf16[256,3072]{1,0:T(8,128)(2,1)} %param.10) | copy-start | bytes 4718596
  7.2 90.3 %all-gather.2.cloned.1.call-start = ((), (), s32[]{:S(2)}) async-start(), calls=%async_computation.3 | async-start | bytes 2981888 | tf_op jit(solution)/shard_map/all_gather | solution.py:56
  9.0 169.0 %reduce-scatter.3.cloned.1.call-start = ((), (), s32[]{:S(2)}) async-start(), calls=%async_computation.2 | async-start | bytes 2609152 | tf_op jit(solution)/shard_map/reduce_scatter | solution.py:46
  10.4 6.6 %copy-start.5 = (bf16[3,3,64,4,64]{4,3,2,1,0:T(4,128)(2,1)}, bf16[3,3,64,4,64]{4,3,2,1,0:T(4,128)(2,1)S(1)}, u32[]{:S(2)}) copy-start(bf16[3,3,64,4,64]{4,3,2,1,0:T(4,128)(2,1)S(1)} %shard_map.90) | copy-start | bytes 884740
  12.6 4.5 %copy-start.3 = (bf16[256,1024]{1,0:T(8,128)(2,1)S(1)}, bf16[256,1024]{1,0:T(8,128)(2,1)}, u32[]{:S(2)}) copy-start(bf16[256,1024]{1,0:T(8,128)(2,1)} %param.8) | copy-start | bytes 1572868
  12.6 33.9 %copy-start.1 = (bf16[1024,256]{1,0:T(8,128)(2,1)S(1)}, bf16[1024,256]{1,0:T(8,128)(2,1)}, u32[]{:S(2)}) copy-start(bf16[1024,256]{1,0:T(8,128)(2,1)} %param.9) | copy-start | bytes 1572868
  51.1 306.3 %reduce-scatter.5.cloned.1.call-start = ((), (), s32[]{:S(2)}) async-start(), calls=%async_computation.4 | async-start | bytes 3194880 | tf_op jit(solution)/shard_map/reduce_scatter | solution.py:66
  102.3 3.6 %copy-start.2 = (bf16[1024,256]{1,0:T(8,128)(2,1)S(1)}, bf16[1024,256]{1,0:T(8,128)(2,1)}, u32[]{:S(2)}) copy-start(bf16[1024,256]{1,0:T(8,128)(2,1)} %param.9) | copy-start | bytes 1572868
  102.3 28.0 %copy-start.4 = (bf16[256,1024]{1,0:T(8,128)(2,1)S(1)}, bf16[256,1024]{1,0:T(8,128)(2,1)}, u32[]{:S(2)}) copy-start(bf16[256,1024]{1,0:T(8,128)(2,1)} %param.8) | copy-start | bytes 1572868
  106.0 26.4 %copy-start.6 = (bf16[3,3,64,4,64]{4,3,2,1,0:T(4,128)(2,1)S(1)}, bf16[3,3,64,4,64]{4,3,2,1,0:T(4,128)(2,1)}, u32[]{:S(2)}) copy-start(bf16[3,3,64,4,64]{4,3,2,1,0:T(4,128)(2,1)} %copy-done.5) | copy-start | bytes 884740
Sparse Core Ops, SparseCore 0:
  10.3 87.0 all-gather.1
  100.6 77.3 reduce-scatter.2
  183.9 173.4 reduce-scatter.4
where the time goes:
time: 368 us; the launch traced here: 364 us
  waiting for transfers between devices  264 us (72%)
  blocking collectives  53 us (14%)
  matrix products  21 us (6%)
  between operations  13.9 us (4%)
  local copies, waits for them, and re-layouts  10.9 us (3%)
    reduce_scatter x1, waiting for transfers between devices, on_device(): lax.psum_scatter(dw_block, 'dp', scatter_dimension=1, tiled=True)  177 us
    all_gather x1, waiting for transfers between devices, on_device(): shard_piece = lax.all_gather(grad_out, 'chan', axis=3, tiled=True)  45.9 us
    reduce_scatter x1, waiting for transfers between devices, on_device(): lax.psum_scatter(lax.dot_general(weight_cols, act_rows, (((0,), (1,)), ((...  40.3 us
    psum x1, blocking collectives, on_device(): lax.psum(jnp.dot(squeezed, se_down.astype(jnp.float32), precision=highest...  29.1 us
    psum x1, blocking collectives, on_device(): lax.psum(jnp.dot(pre_grad, se_up.astype(jnp.float32).T, precision=highest...  23.9 us
    conv_general_dilated x2, matrix products, grouped(): lax.conv_general_dilated(inputs, kernel, (1, 1), 'SAME', dimension_number...  8.66 us
  transfers between devices with their start and end apart: 3, of which 3 were waited for; matrix products, arithmetic and copies ran while one was open for 9% of the time, Pallas kernels for 0%

commit v1 on v0

v1 whole, which is shorter than its diff:
```python
import jax
import jax.numpy as jnp
from jax import lax
from jax.experimental import pallas as pl
from jax.experimental.pallas import tpu as pltpu
from jax.sharding import PartitionSpec as P

BF = jnp.bfloat16
F32 = jnp.float32

NX, NZL, NZH, NY, NC = 4, 3, 4, 8, 2
CELLS = 196
ROWS = 400
VALID = 392
CH = 256
SLAB = 768
SE = 1024
OWN = 48
HALF = {1: (0, 208), -1: (208, 192)}


class Sems:
    def __init__(self, send, recv):
        self.send, self.recv, self.n_send, self.n_recv = send, recv, 0, 0

    def take(self, count=1):
        at = self.n_send
        self.n_send += count
        return at


def dot(a, b):
    return lax.dot_general(a, b, (((1,), (0,)), ((), ())), preferred_element_type=F32)


def dot_nt(a, b):
    return lax.dot_general(a, b, (((1,), (1,)), ((), ())), preferred_element_type=F32)


def dot_tn(a, b):
    return lax.dot_general(a, b, (((0,), (0,)), ((), ())), preferred_element_type=F32)


def sigmoid(v):
    return jax.nn.sigmoid(v)


def silu_grad(v):
    s = sigmoid(v)
    return s * (1.0 + v * (1.0 - s))


def split3(v):
    hi = v.astype(BF).astype(F32)
    rest = v - hi
    mid = rest.astype(BF).astype(F32)
    lo = (rest - mid).astype(BF).astype(F32)
    return jnp.concatenate([hi, mid, lo, jnp.zeros_like(hi)], axis=0).astype(BF)


def join3(r):
    return r[0:2] + r[2:4] + r[4:6]


def per_image(g):
    return jnp.concatenate([g, g, g, g], axis=0)


def scale_rows(v, g8):
    return (v.reshape(ROWS // 8, 8, CH) * g8[None]).reshape(ROWS, CH)


def image_sums(v):
    s = jnp.sum(v.reshape(ROWS // 8, 8, CH), axis=0)
    return s[0:2] + s[2:4] + s[4:6] + s[6:8]


def taps(x):
    row = lax.broadcasted_iota(jnp.int32, (ROWS, CH), 0)
    cell = row >> 1
    w = cell - 14 * ((cell * 4682) >> 16)
    cols = [
        jnp.where(w >= 1, pltpu.roll(x, 2, 0), 0.0),
        x,
        jnp.where(w <= 12, pltpu.roll(x, ROWS - 2, 0), 0.0),
    ]
    out = []
    for dy in range(3):
        for c in cols:
            if dy == 0:
                c = jnp.where(row >= 28, pltpu.roll(c, 28, 0), 0.0)
            elif dy == 2:
                c = jnp.where(row < VALID - 28, pltpu.roll(c, ROWS - 28, 0), 0.0)
            out.append(c.astype(BF))
    return jnp.concatenate(out, axis=1)


def kernel(
    hid_h, cw_h, down_h, up_h, w_h, g_h,
    proj_o, gh_o, gp_o,
    hid_v, cw_v, down_v, up_v, bd, conv_v, act_v,
    gs, wg, wrel, xs, se1, se2,
    p32, psend, precv,
    qown, qnear, qsend, qrel, qdir, qcomb, qcs,
    dw, cs, cr, dsum, ysend, yrecv, zsend, zrecv,
    proj_v, gh_v, gp_v,
    lsem, osem, ssem, rsem,
):
    dp = lax.axis_index("dp")
    ch = lax.axis_index("chan")
    core = dp % NC
    y = (dp // NC) % NY
    zh = dp // (NC * NY)
    x = ch // NZL
    zl = ch % NZL

    def dev(x_=x, zl_=zl, zh_=zh, y_=y, core_=core):
        return {"dp": (zh_ * NY + y_) * NC + core_, "chan": x_ * NZL + zl_}

    counter = [0]
    sends = []

    def rcopy(src, dst, to, key=None):
        i = counter[0]
        counter[0] += 1
        c = pltpu.make_async_remote_copy(
            src_ref=src, dst_ref=dst, send_sem=ssem.at[i], recv_sem=rsem.at[i],
            device_id=to, device_id_type=pl.DeviceIdType.MESH,
        )
        return c

    def go(c):
        c.start()
        sends.append(c)
        return c

    xp = {1: (x + 1) % NX, -1: (x + NX - 1) % NX, 2: (x + 2) % NX}
    core2 = 1 - core
    slab0 = pl.multiple_of(x * SLAB, SLAB)
    r0 = pl.multiple_of(core * 128, 128)

    loads = {}
    for i, (name, src, dst) in enumerate((
        ("hid", hid_h, hid_v), ("cw", cw_h, cw_v), ("down", down_h, down_v),
        ("up", up_h, up_v), ("g", g_h, gs.at[zl]),
        ("w", w_h.at[:, pl.ds(slab0, SLAB)], wg.at[x]),
    )):
        loads[name] = pltpu.make_async_copy(src, dst, lsem.at[i])
        loads[name].start()

    barrier = pltpu.get_barrier_semaphore()

    def greet(to):
        pl.semaphore_signal(barrier, inc=1, device_id=to, device_id_type=pl.DeviceIdType.MESH)

    for k in range(1, NX * NZL):
        greet({"dp": dp, "chan": (ch + k) % (NX * NZL)})
    greet(dev(core_=core2))
    greet(dev(y_=(y + 1) % NY))
    greet(dev(y_=(y + NY - 1) % NY))
    for h in range(NZH):
        greet(dev(x_=zh, zh_=h))

    loads["hid"].wait()
    loads["cw"].wait()
    ri = lax.broadcasted_iota(jnp.int32, (CH, CH), 0) >> 6
    ci = lax.broadcasted_iota(jnp.int32, (CH, CH), 1) >> 6
    for t in range(9):
        k = cw_v[t // 3, t % 3].astype(F32)
        k = jnp.concatenate([k, k, k, k], axis=0)
        bd[t] = jnp.where(ri == ci, k, 0.0).astype(BF)
    row = lax.broadcasted_iota(jnp.int32, (ROWS, CH), 0)
    conv = dot(taps(hid_v[...].astype(F32)), bd[...].reshape(9 * CH, CH))
    conv = jnp.where(row < VALID, conv, 0.0)
    conv_v[...] = conv
    act = (conv * sigmoid(conv)).astype(BF)
    act_v[...] = act
    squeezed = image_sums(act.astype(F32)) * (1.0 / CELLS)
    loads["down"].wait()
    se1[ch] = join3(dot(split3(squeezed), down_v[...]))

    pl.semaphore_wait(barrier, NX * NZL - 1 + 3 + NZH)

    def se_push(buf):
        out = []
        for k in range(1, NX * NZL):
            out.append(go(rcopy(buf.at[ch], buf.at[ch], {"dp": dp, "chan": (ch + k) % (NX * NZL)})))
        return out

    se_copies = se_push(se1)

    w_rel, w_near = {}, {}
    for d in (1, -1):
        at = 0 if d == 1 else 1
        far = pl.multiple_of(xp[2] * SLAB, SLAB)
        w_rel[d] = go(rcopy(
            w_h.at[pl.ds(pl.multiple_of(r0 + 64 * at, 64), 64), pl.ds(far, SLAB)],
            wrel.at[at], dev(x_=xp[d])))
    for d in (1, -1):
        near = pl.multiple_of(xp[d] * SLAB, SLAB)
        w_near[d] = go(rcopy(
            w_h.at[pl.ds(r0, 128), pl.ds(near, SLAB)],
            wg.at[x, pl.ds(r0, 128), :], dev(x_=xp[d])))

    g_copies = []
    loads["g"].wait()
    for k in range(1, NZL):
        g_copies.append(go(rcopy(gs.at[zl], gs.at[zl], dev(zl_=(zl + k) % NZL))))

    w_fwd = {}
    for d in (1, -1):
        at = 0 if d == 1 else 1
        w_rel[d].wait_recv()
        w_fwd[d] = go(rcopy(
            wrel.at[at],
            wg.at[xp[-d], pl.ds(pl.multiple_of(r0 + 64 * at, 64), 64), :],
            dev(x_=xp[d])))

    loads["up"].wait()
    for c in se_copies:
        c.wait_recv()
    pre = se1[0]
    for k in range(1, NX * NZL):
        pre = pre + se1[k]
    gating = sigmoid(join3(dot(split3(pre * sigmoid(pre)), up_v[...])))
    g8 = per_image(gating)
    xs[x] = scale_rows(act_v[...].astype(F32), g8).astype(BF)

    x_first, x_rest, x_fwd = {}, {}, {}
    for d in (1, -1):
        a, n = HALF[d]
        x_first[d] = go(rcopy(xs.at[x, pl.ds(a, n), :], xs.at[x, pl.ds(a, n), :], dev(x_=xp[d])))
    for d in (1, -1):
        a, n = HALF[-d]
        x_rest[d] = go(rcopy(xs.at[x, pl.ds(a, n), :], xs.at[x, pl.ds(a, n), :], dev(x_=xp[d])))

    w_sib = []
    for d in (1, -1):
        w_near[d].wait_recv()
        ref = wg.at[xp[-d], pl.ds(r0, 128), :]
        w_sib.append(go(rcopy(ref, ref, dev(core_=core2))))
    for d in (1, -1):
        at = 0 if d == 1 else 1
        w_fwd[d].wait_recv()
        ref = wg.at[xp[2], pl.ds(pl.multiple_of(r0 + 64 * at, 64), 64), :]
        w_sib.append(go(rcopy(ref, ref, dev(core_=core2))))

    for c in g_copies:
        c.wait_recv()

    for d in (1, -1):
        a, n = HALF[d]
        x_first[d].wait_recv()
        ref = xs.at[xp[-d], pl.ds(a, n), :]
        x_fwd[d] = go(rcopy(ref, ref, dev(x_=xp[d])))

    gcat = jnp.concatenate([gs[0], gs[1], gs[2]], axis=1)
    subs = (x, xp[-1], xp[1], xp[2])

    c_copies = []

    def weight_grad(j):
        dw[j] = dot_tn(gcat, xs[subs[j]]).reshape(NY, NC, OWN, CH)
        cs[j] = dw[j, :, core2].astype(BF)
        c_copies.append(go(rcopy(cs.at[j], cr.at[j], dev(core_=core2))))

    y_dir = lambda j: -1 if j % 2 == 0 else 1
    y_last = {}

    def y_step(j, s):
        for long in (True, False):
            hops = 4 if long else 3
            if s > hops:
                continue
            e = y_dir(j) if long else -y_dir(j)
            base = 0 if long else 4
            owner = (y + e * (hops + 1 - s) + NY) % NY
            v = dsum[j, owner]
            if s > 1:
                y_last[j, long].wait_recv()
                v = v + yrecv[j, base + s - 2].astype(F32)
            ysend[j, base + s - 1] = v.astype(BF)
            y_last[j, long] = go(rcopy(
                ysend.at[j, base + s - 1], yrecv.at[j, base + s - 1], dev(y_=(y + e + NY) % NY)))

    def core_sum(j):
        c_copies[j].wait_recv()
        dsum[j] = dw[j, :, core] + cr[j].astype(F32)

    weight_grad(0)

    for c in w_sib:
        c.wait_recv()
    loads["w"].wait()

    def q_part(xi):
        return dot_nt(gcat, wg[xi])

    q_rel, q_dir, q_comb = {}, {}, {}
    qsend[0] = q_part(xp[2]).astype(BF)
    for d in (1, -1):
        a, n = HALF[d]
        q_rel[d] = go(rcopy(
            qsend.at[0, pl.ds(a, n), :], qrel.at[pl.ds(a, n), :], dev(x_=xp[d])))
    for d in (1, -1):
        at = 0 if d == 1 else 1
        a, n = HALF[d]
        b, m = HALF[-d]
        part = q_part(xp[d])
        qsend[1 + at] = part.astype(BF)
        qnear[pl.ds(a, n), :] = part[a:a + n]
        q_dir[d] = go(rcopy(
            qsend.at[1 + at, pl.ds(b, m), :], qdir.at[pl.ds(b, m), :], dev(x_=xp[d])))
    qown[...] = q_part(x)
    core_sum(0)
    y_step(0, 1)
    for d in (1, -1):
        a, n = HALF[d]
        q_rel[d].wait_recv()
        qcs[pl.ds(a, n), :] = (qnear[pl.ds(a, n), :] + qrel[pl.ds(a, n), :].astype(F32)).astype(BF)
        q_comb[d] = go(rcopy(
            qcs.at[pl.ds(a, n), :], qcomb.at[pl.ds(a, n), :], dev(x_=xp[d])))

    for j, d in ((1, 1), (2, -1)):
        x_rest[d].wait_recv()
        weight_grad(j)
    y_step(0, 2)
    for j in (1, 2):
        core_sum(j)
        y_step(j, 1)
    for d in (1, -1):
        x_fwd[d].wait_recv()
    weight_grad(3)

    xcat = jnp.concatenate([xs[0], xs[1], xs[2], xs[3]], axis=1)
    wcat = wg[...].reshape(NX * CH, SLAB)
    for zo in range(NZL):
        part = dot(xcat, wcat[:, zo * CH:(zo + 1) * CH])
        p32[zo] = part
        psend[zo] = part.astype(BF)
    p_copies = []
    for k in range(1, NZL):
        p_copies.append(go(rcopy(
            psend.at[(zl + k) % NZL], precv.at[k - 1], dev(zl_=(zl + k) % NZL))))

    core_sum(3)
    y_step(3, 1)
    y_step(0, 3)
    y_step(1, 2)
    y_step(2, 2)

    for d in (1, -1):
        q_dir[d].wait_recv()
        q_comb[d].wait_recv()
    qown[...] = qown[...] + qdir[...].astype(F32) + qcomb[...].astype(F32)
    gate_grad = image_sums(qown[...] * act_v[...].astype(F32))
    pre_grad = gate_grad * gating * (1.0 - gating)
    se2[ch] = join3(dot_nt(split3(pre_grad), up_v[...]))
    se_copies = se_push(se2)

    y_step(3, 2)
    y_step(0, 4)
    y_step(1, 3)
    y_step(2, 3)
    y_step(3, 3)
    y_step(1, 4)
    y_step(2, 4)
    y_step(3, 4)

    itself = zh == x
    z_base = counter[0]
    counter[0] += NZH
    z_self = []
    zt_base = z_base

    def z_copy(j, to_x):
        return pltpu.make_async_remote_copy(
            src_ref=zsend.at[j], dst_ref=zrecv.at[zh],
            send_sem=ssem.at[zt_base + j], recv_sem=rsem.at[zt_base + zh],
            device_id=dev(x_=to_x, zh_=x), device_id_type=pl.DeviceIdType.MESH)

    for j in range(4):
        y_last[j, True].wait_recv()
        y_last[j, False].wait_recv()
        total = dsum[j, y] + yrecv[j, 3].astype(F32) + yrecv[j, 6].astype(F32)
        zsend[j] = total.astype(BF)
        if j == 0:
            @pl.when(itself)
            def _():
                zrecv[zh] = zsend[0]

            @pl.when(jnp.logical_not(itself))
            def _():
                z_copy(0, subs[0]).start()
        else:
            go(z_copy(j, subs[j]))

    for c in se_copies:
        c.wait_recv()
    ex = se2[0]
    for k in range(1, NX * NZL):
        ex = ex + se2[k]
    pre = se1[0]
    for k in range(1, NX * NZL):
        pre = pre + se1[k]
    ex = ex * silu_grad(pre)
    sq8 = per_image(join3(dot_nt(split3(ex), down_v[...])) * (1.0 / CELLS))
    act_grad = scale_rows(qown[...], g8).reshape(ROWS // 8, 8, CH) + sq8[None]
    conv_grad = act_grad.reshape(ROWS, CH) * silu_grad(conv_v[...])
    conv_grad = conv_grad.astype(BF).astype(F32)
    turned = jnp.concatenate([bd[8 - t] for t in range(9)], axis=1)
    gh_v[...] = dot_nt(taps(conv_grad), turned).astype(BF)
    gh_copy = pltpu.make_async_copy(gh_v, gh_o, osem.at[0])
    gh_copy.start()

    for c in p_copies:
        c.wait_recv()
    proj = p32[zl] + precv[0].astype(F32) + precv[1].astype(F32)
    proj_v[...] = proj.astype(BF)
    proj_copy = pltpu.make_async_copy(proj_v, proj_o, osem.at[1])
    proj_copy.start()

    for h in range(NZH):
        @pl.when(jnp.logical_not(jnp.logical_and(itself, zh == h)))
        def _():
            pltpu.make_async_remote_copy(
                src_ref=zsend.at[0], dst_ref=zrecv.at[h],
                send_sem=ssem.at[zt_base], recv_sem=rsem.at[zt_base + h],
                device_id=dev(x_=subs[0], zh_=x), device_id_type=pl.DeviceIdType.MESH,
            ).wait_recv()
    gp = zrecv[0].astype(F32)
    for h in range(1, NZH):
        gp = gp + zrecv[h].astype(F32)
    gp_v[...] = gp
    gp_copy = pltpu.make_async_copy(gp_v, gp_o, osem.at[2])
    gp_copy.start()

    for c in sends:
        c.wait_send()

    @pl.when(jnp.logical_not(itself))
    def _():
        z_copy(0, subs[0]).wait_send()

    gh_copy.wait()
    proj_copy.wait()
    gp_copy.wait()


def on_device(hidden, conv_weight, se_down, se_up, proj_weight, grad_out):
    def rows_of(v):
        v = jnp.transpose(v, (1, 2, 0, 3)).reshape(VALID, CH)
        return jnp.pad(v, ((0, ROWS - VALID), (0, 0)))

    def images_of(v):
        return jnp.transpose(v[:VALID].reshape(14, 14, 2, CH), (2, 0, 1, 3))

    V = pltpu.VMEM
    n_copies = 130
    any_spec = pl.BlockSpec(memory_space=pl.ANY)
    proj, gh, gp = pl.pallas_call(
        kernel,
        out_shape=(
            jax.ShapeDtypeStruct((ROWS, CH), BF),
            jax.ShapeDtypeStruct((ROWS, CH), BF),
            jax.ShapeDtypeStruct((OWN, CH), F32),
        ),
        in_specs=[any_spec] * 6,
        out_specs=(any_spec,) * 3,
        scratch_shapes=[
            V((ROWS, CH), BF), V((3, 3, 64, CH), BF), V((CH, SE), BF), V((SE, CH), BF),
            V((9, CH, CH), BF), V((ROWS, CH), F32), V((ROWS, CH), BF),
            V((NZL, ROWS, CH), BF), V((NX, CH, SLAB), BF), V((2, 64, SLAB), BF),
            V((NX, ROWS, CH), BF), V((NX * NZL, 2, SE), F32), V((NX * NZL, 2, SE), F32),
            V((NZL, ROWS, CH), F32), V((NZL, ROWS, CH), BF), V((2, ROWS, CH), BF),
            V((ROWS, CH), F32), V((ROWS, CH), F32), V((3, ROWS, CH), BF),
            V((ROWS, CH), BF), V((ROWS, CH), BF), V((ROWS, CH), BF), V((ROWS, CH), BF),
            V((4, NY, NC, OWN, CH), F32), V((4, NY, OWN, CH), BF), V((4, NY, OWN, CH), BF),
            V((4, NY, OWN, CH), F32), V((4, 7, OWN, CH), BF), V((4, 7, OWN, CH), BF),
            V((4, OWN, CH), BF), V((NZH, OWN, CH), BF),
            V((ROWS, CH), BF), V((ROWS, CH), BF), V((OWN, CH), F32),
            pltpu.SemaphoreType.DMA((6,)), pltpu.SemaphoreType.DMA((3,)),
            pltpu.SemaphoreType.DMA((n_copies,)), pltpu.SemaphoreType.DMA((n_copies,)),
        ],
        compiler_params=pltpu.CompilerParams(
            collective_id=0, has_side_effects=True, vmem_limit_bytes=60 * 2**20
        ),
        name="block",
    )(rows_of(hidden), conv_weight, se_down, se_up, proj_weight, rows_of(grad_out))
    return images_of(proj), images_of(gh), gp.T


def solution(mesh):
    in_specs = (
        P("dp", None, None, "chan"),
        P(None, None, None, "chan"),
        P("chan", None),
        P(None, "chan"),
        P("chan", None),
        P("dp", None, None, "chan"),
    )
    out_specs = (P("dp", None, None, "chan"), P("dp", None, None, "chan"), P("chan", "dp"))
    return jax.shard_map(
        on_device, mesh=mesh, in_specs=in_specs, out_specs=out_specs, check_vma=False
    )
```

time: 368 us -> 76.2 us (0.21)
  the two profiles are of different devices: /device:TPU:1 before, /device:TPU:4 now
where the time goes in v1:
time: 76.2 us; the launch traced here: 76 us
  Pallas kernels  67.9 us (89%)
  local copies, waits for them, and re-layouts  7.44 us (10%)
    pallas_call x1, Pallas kernels, on_device(): pl.pallas_call(kernel, out_shape=(jax.ShapeDtypeStruct((ROWS, CH), BF), j...  67.9 us
    reshape x2, local copies, waits for them, and re-layouts, rows_of(): v = jnp.transpose(v, (1, 2, 0, 3)).reshape(VALID, CH)  2.02 us
    slice x2, local copies, waits for them, and re-layouts, images_of(): return jnp.transpose(v[:VALID].reshape(14, 14, 2, CH), (2, 0, 1, 3))  1.9 us

profile of v1, /device:TPU:4, one launch (start us, length us, event | category | flops | bytes accessed | tf_op | source)
XLA Modules:
  0.0 76.0 jit_solution(8887494158829326851)
XLA Ops:
  0.6 1.0 %reshape.18 = bf16[392,256]{1,0:T(8,128)(2,1)S(1)} reshape(bf16[14,14,2,256]{3,2,1,0:T(2,128)(2,1)} %bitcast.5) | data formatting | bytes 401408 | tf_op jit(solution)/shard_map/reshape | solution.py:452
  1.6 0.7 pad.7.hid_h
  2.3 1.0 %reshape.19 = bf16[392,256]{1,0:T(8,128)(2,1)S(1)} reshape(bf16[14,14,2,256]{3,2,1,0:T(2,128)(2,1)} %bitcast.6) | data formatting | bytes 401408 | tf_op jit(solution)/shard_map/reshape | solution.py:452
  3.3 0.7 pad.8.g_h
  4.0 67.9 %block.1 = (bf16[400,256]{1,0:T(8,128)(2,1)}, bf16[400,256]{1,0:T(8,128)(2,1)}, f32[48,256]{1,0:T(8,128)}) custom-call(bf16[400,256]{1,0:T(8,128)(2,1)} %pad.7.hid_h, bf16[3,3,64,256]{3,2,1,0:T(8,128)(2,1)} %cw_h.1, bf16[256,1024]{1,0:T(8,128)(2,1)} %down_h.1, bf16[1024,256]{1,0:T(8,128)(2,1)} %up_h.1, bf16[256,3072]{1,0:T(8,128)(2,1)} %w_h.1, ...), custom_call_target="tpu_custom_call" | custom-call | tf_op jit(solution)/shard_map/block/pallas_call | solution.py:461
  71.9 0.0 copy-start
  72.0 1.0 %slice.6 = bf16[392,256]{1,0:T(8,128)(2,1)S(1)} slice(bf16[400,256]{1,0:T(8,128)(2,1)} %get-tuple-element.6), slice={[0:392], [0:256]} | slice | bytes 401408 | tf_op jit(solution)/shard_map/slice | solution.py:456
  72.9 0.8 reshape.20
  73.7 0.9 %slice.7 = bf16[392,256]{1,0:T(8,128)(2,1)S(1)} slice(bf16[400,256]{1,0:T(8,128)(2,1)} %get-tuple-element.7), slice={[0:392], [0:256]} | slice | bytes 401408 | tf_op jit(solution)/shard_map/slice | solution.py:456
  74.6 0.8 reshape.21
  75.4 0.0 copy-done
  75.4 0.6 copy.10
Async XLA Ops:
  71.9 3.4 %copy-start = (f32[48,256]{1,0:T(8,128)S(1)}, f32[48,256]{1,0:T(8,128)}, u32[]{:S(2)}) copy-start(f32[48,256]{1,0:T(8,128)} %get-tuple-element.8) | copy-start | bytes 147460

commit v2 on v1

--- a/solution.py
+++ b/solution.py
@@ -73,6 +73,10 @@
 def image_sums(v):
     s = jnp.sum(v.reshape(ROWS // 8, 8, CH), axis=0)
     return s[0:2] + s[2:4] + s[4:6] + s[6:8]
+
+
+def rows_of(v):
+    return jnp.concatenate([v.reshape(VALID, CH), jnp.zeros((ROWS - VALID, CH), v.dtype)], axis=0)
 
 
 def taps(x):
@@ -99,7 +103,7 @@
     hid_h, cw_h, down_h, up_h, w_h, g_h,
     proj_o, gh_o, gp_o,
     hid_v, cw_v, down_v, up_v, bd, conv_v, act_v,
-    gs, wg, wrel, xs, se1, se2,
+    graw, gs, gt, wg, wrel, xs, se1, se2,
     p32, psend, precv,
     qown, qnear, qsend, qrel, qdir, qcomb, qcs,
     dw, cs, cr, dsum, ysend, yrecv, zsend, zrecv,
@@ -142,7 +146,7 @@
     loads = {}
     for i, (name, src, dst) in enumerate((
         ("hid", hid_h, hid_v), ("cw", cw_h, cw_v), ("down", down_h, down_v),
-        ("up", up_h, up_v), ("g", g_h, gs.at[zl]),
+        ("up", up_h, up_v), ("g", g_h, graw.at[zl]),
         ("w", w_h.at[:, pl.ds(slab0, SLAB)], wg.at[x]),
     )):
         loads[name] = pltpu.make_async_copy(src, dst, lsem.at[i])
@@ -170,7 +174,7 @@
         k = jnp.concatenate([k, k, k, k], axis=0)
         bd[t] = jnp.where(ri == ci, k, 0.0).astype(BF)
     row = lax.broadcasted_iota(jnp.int32, (ROWS, CH), 0)
-    conv = dot(taps(hid_v[...].astype(F32)), bd[...].reshape(9 * CH, CH))
+    conv = dot(taps(rows_of(hid_v[...].astype(F32))), bd[...].reshape(9 * CH, CH))
     conv = jnp.where(row < VALID, conv, 0.0)
     conv_v[...] = conv
     act = (conv * sigmoid(conv)).astype(BF)
@@ -196,16 +200,17 @@
         w_rel[d] = go(rcopy(
             w_h.at[pl.ds(pl.multiple_of(r0 + 64 * at, 64), 64), pl.ds(far, SLAB)],
             wrel.at[at], dev(x_=xp[d])))
-    for d in (1, -1):
+    def w_near_copy(d, part):
         near = pl.multiple_of(xp[d] * SLAB, SLAB)
-        w_near[d] = go(rcopy(
-            w_h.at[pl.ds(r0, 128), pl.ds(near, SLAB)],
-            wg.at[x, pl.ds(r0, 128), :], dev(x_=xp[d])))
+        rows = pl.ds(pl.multiple_of(r0 + 64 * part, 64), 64)
+        return go(rcopy(w_h.at[rows, pl.ds(near, SLAB)], wg.at[x, rows, :], dev(x_=xp[d])))
+
+    for d in (1, -1):
+        w_near[d, 0] = w_near_copy(d, 0)
 
     g_copies = []
-    loads["g"].wait()
     for k in range(1, NZL):
-        g_copies.append(go(rcopy(gs.at[zl], gs.at[zl], dev(zl_=(zl + k) % NZL))))
+        g_copies.append(go(rcopy(g_h, graw.at[zl], dev(zl_=(zl + k) % NZL))))
 
     w_fwd = {}
     for d in (1, -1):
@@ -234,33 +239,40 @@
         a, n = HALF[-d]
         x_rest[d] = go(rcopy(xs.at[x, pl.ds(a, n), :], xs.at[x, pl.ds(a, n), :], dev(x_=xp[d])))
 
-    w_sib = []
-    for d in (1, -1):
-        w_near[d].wait_recv()
-        ref = wg.at[xp[-d], pl.ds(r0, 128), :]
-        w_sib.append(go(rcopy(ref, ref, dev(core_=core2))))
-    for d in (1, -1):
-        at = 0 if d == 1 else 1
-        w_fwd[d].wait_recv()
-        ref = wg.at[xp[2], pl.ds(pl.multiple_of(r0 + 64 * at, 64), 64), :]
-        w_sib.append(go(rcopy(ref, ref, dev(core_=core2))))
-
-    for c in g_copies:
-        c.wait_recv()
-
     for d in (1, -1):
         a, n = HALF[d]
         x_first[d].wait_recv()
         ref = xs.at[xp[-d], pl.ds(a, n), :]
         x_fwd[d] = go(rcopy(ref, ref, dev(x_=xp[d])))
+    for d in (1, -1):
+        w_near[d, 1] = w_near_copy(d, 1)
+
+    w_sib = []
+
+    def w_share(copy, slot, part):
+        copy.wait_recv()
+        ref = wg.at[slot, pl.ds(pl.multiple_of(r0 + 64 * part, 64), 64), :]
+        w_sib.append(go(rcopy(ref, ref, dev(core_=core2))))
+
+    for d in (1, -1):
+        w_share(w_near[d, 0], xp[-d], 0)
+    for d in (1, -1):
+        w_share(w_fwd[d], xp[2], 0 if d == 1 else 1)
+
+    loads["g"].wait()
+    for c in g_copies:
+        c.wait_recv()
+    for z in range(NZL):
+        gs[z] = rows_of(graw[z].astype(F32)).astype(BF)
 
     gcat = jnp.concatenate([gs[0], gs[1], gs[2]], axis=1)
+    gt[...] = gcat.T
     subs = (x, xp[-1], xp[1], xp[2])
 
     c_copies = []
 
     def weight_grad(j):
-        dw[j] = dot_tn(gcat, xs[subs[j]]).reshape(NY, NC, OWN, CH)
+        dw[j] = dot(gt[...], xs[subs[j]]).reshape(NY, NC, OWN, CH)
         cs[j] = dw[j, :, core2].astype(BF)
         c_copies.append(go(rcopy(cs.at[j], cr.at[j], dev(core_=core2))))
 
@@ -287,12 +299,62 @@
         c_copies[j].wait_recv()
         dsum[j] = dw[j, :, core] + cr[j].astype(F32)
 
+    itself = zh == x
+    z_base = counter[0]
+    counter[0] += NZH
+
+    def z_copy(j, to_x):
+        return pltpu.make_async_remote_copy(
+            src_ref=zsend.at[j], dst_ref=zrecv.at[zh],
+            send_sem=ssem.at[z_base + j], recv_sem=rsem.at[z_base + zh],
+            device_id=dev(x_=to_x, zh_=x), device_id_type=pl.DeviceIdType.MESH)
+
+    def z_push(j):
+        y_last[j, True].wait_recv()
+        y_last[j, False].wait_recv()
+        total = dsum[j, y] + yrecv[j, 3].astype(F32) + yrecv[j, 6].astype(F32)
+        zsend[j] = total.astype(BF)
+        if j == 0:
+            @pl.when(itself)
+            def _():
+                zrecv[zh] = zsend[0]
+
+            @pl.when(jnp.logical_not(itself))
+            def _():
+                z_copy(0, subs[0]).start()
+        else:
+            go(z_copy(j, subs[j]))
+
     weight_grad(0)
-
+    x_rest[1].wait_recv()
+    weight_grad(1)
+    core_sum(0)
+    y_step(0, 1)
+    x_rest[-1].wait_recv()
+    weight_grad(2)
+    for d in (1, -1):
+        x_fwd[d].wait_recv()
+    weight_grad(3)
+    for j in (1, 2):
+        core_sum(j)
+        y_step(j, 1)
+    y_step(0, 2)
+
+    loads["w"].wait()
+    xcat = jnp.concatenate([xs[0], xs[1], xs[2], xs[3]], axis=1)
+    for d in (1, -1):
+        w_share(w_near[d, 1], xp[-d], 1)
     for c in w_sib:
         c.wait_recv()
-    loads["w"].wait()
-
+    wcat = wg[...].reshape(NX * CH, SLAB)
+    for zo in range(NZL):
+        part = dot(xcat, wcat[:, zo * CH:(zo + 1) * CH])
+        p32[zo] = part
+        psend[zo] = part.astype(BF)
+    p_copies = []
+    for k in range(1, NZL):
+        p_copies.append(go(rcopy(
+            psend.at[(zl + k) % NZL], precv.at[k - 1], dev(zl_=(zl + k) % NZL))))
     def q_part(xi):
         return dot_nt(gcat, wg[xi])
 
@@ -312,8 +374,17 @@
         q_dir[d] = go(rcopy(
             qsend.at[1 + at, pl.ds(b, m), :], qdir.at[pl.ds(b, m), :], dev(x_=xp[d])))
     qown[...] = q_part(x)
-    core_sum(0)
-    y_step(0, 1)
+    core_sum(3)
+    y_step(3, 1)
+    y_step(1, 2)
+    y_step(2, 2)
+    y_step(0, 3)
+    y_step(3, 2)
+    y_step(0, 4)
+    y_step(1, 3)
+    y_step(2, 3)
+    y_step(3, 3)
+    z_push(0)
     for d in (1, -1):
         a, n = HALF[d]
         q_rel[d].wait_recv()
@@ -321,34 +392,12 @@
         q_comb[d] = go(rcopy(
             qcs.at[pl.ds(a, n), :], qcomb.at[pl.ds(a, n), :], dev(x_=xp[d])))
 
-    for j, d in ((1, 1), (2, -1)):
-        x_rest[d].wait_recv()
-        weight_grad(j)
-    y_step(0, 2)
-    for j in (1, 2):
-        core_sum(j)
-        y_step(j, 1)
-    for d in (1, -1):
-        x_fwd[d].wait_recv()
-    weight_grad(3)
-
-    xcat = jnp.concatenate([xs[0], xs[1], xs[2], xs[3]], axis=1)
-    wcat = wg[...].reshape(NX * CH, SLAB)
-    for zo in range(NZL):
-        part = dot(xcat, wcat[:, zo * CH:(zo + 1) * CH])
-        p32[zo] = part
-        psend[zo] = part.astype(BF)
-    p_copies = []
-    for k in range(1, NZL):
-        p_copies.append(go(rcopy(
-            psend.at[(zl + k) % NZL], precv.at[k - 1], dev(zl_=(zl + k) % NZL))))
-
-    core_sum(3)
-    y_step(3, 1)
-    y_step(0, 3)
-    y_step(1, 2)
-    y_step(2, 2)
-
+    y_step(1, 4)
+    y_step(2, 4)
+    y_step(3, 4)
+    z_push(1)
+    z_push(2)
+    z_push(3)
     for d in (1, -1):
         q_dir[d].wait_recv()
         q_comb[d].wait_recv()
@@ -358,42 +407,13 @@
     se2[ch] = join3(dot_nt(split3(pre_grad), up_v[...]))
     se_copies = se_push(se2)
 
-    y_step(3, 2)
-    y_step(0, 4)
-    y_step(1, 3)
-    y_step(2, 3)
-    y_step(3, 3)
-    y_step(1, 4)
-    y_step(2, 4)
-    y_step(3, 4)
-
-    itself = zh == x
-    z_base = counter[0]
-    counter[0] += NZH
-    z_self = []
-    zt_base = z_base
-
-    def z_copy(j, to_x):
-        return pltpu.make_async_remote_copy(
-            src_ref=zsend.at[j], dst_ref=zrecv.at[zh],
-            send_sem=ssem.at[zt_base + j], recv_sem=rsem.at[zt_base + zh],
-            device_id=dev(x_=to_x, zh_=x), device_id_type=pl.DeviceIdType.MESH)
-
-    for j in range(4):
-        y_last[j, True].wait_recv()
-        y_last[j, False].wait_recv()
-        total = dsum[j, y] + yrecv[j, 3].astype(F32) + yrecv[j, 6].astype(F32)
-        zsend[j] = total.astype(BF)
-        if j == 0:
-            @pl.when(itself)
-            def _():
-                zrecv[zh] = zsend[0]
-
-            @pl.when(jnp.logical_not(itself))
-            def _():
-                z_copy(0, subs[0]).start()
-        else:
-            go(z_copy(j, subs[j]))
+
+    for c in p_copies:
+        c.wait_recv()
+    proj = p32[zl] + precv[0].astype(F32) + precv[1].astype(F32)
+    proj_v[...] = proj.astype(BF)
+    proj_copy = pltpu.make_async_copy(proj_v.at[pl.ds(0, VALID), :], proj_o, osem.at[1])
+    proj_copy.start()
 
     for c in se_copies:
         c.wait_recv()
@@ -410,22 +430,15 @@
     conv_grad = conv_grad.astype(BF).astype(F32)
     turned = jnp.concatenate([bd[8 - t] for t in range(9)], axis=1)
     gh_v[...] = dot_nt(taps(conv_grad), turned).astype(BF)
-    gh_copy = pltpu.make_async_copy(gh_v, gh_o, osem.at[0])
+    gh_copy = pltpu.make_async_copy(gh_v.at[pl.ds(0, VALID), :], gh_o, osem.at[0])
     gh_copy.start()
-
-    for c in p_copies:
-        c.wait_recv()
-    proj = p32[zl] + precv[0].astype(F32) + precv[1].astype(F32)
-    proj_v[...] = proj.astype(BF)
-    proj_copy = pltpu.make_async_copy(proj_v, proj_o, osem.at[1])
-    proj_copy.start()
 
     for h in range(NZH):
         @pl.when(jnp.logical_not(jnp.logical_and(itself, zh == h)))
         def _():
             pltpu.make_async_remote_copy(
                 src_ref=zsend.at[0], dst_ref=zrecv.at[h],
-                send_sem=ssem.at[zt_base], recv_sem=rsem.at[zt_base + h],
+                send_sem=ssem.at[z_base], recv_sem=rsem.at[z_base + h],
                 device_id=dev(x_=subs[0], zh_=x), device_id_type=pl.DeviceIdType.MESH,
             ).wait_recv()
     gp = zrecv[0].astype(F32)
@@ -448,12 +461,11 @@
 
 
 def on_device(hidden, conv_weight, se_down, se_up, proj_weight, grad_out):
-    def rows_of(v):
-        v = jnp.transpose(v, (1, 2, 0, 3)).reshape(VALID, CH)
-        return jnp.pad(v, ((0, ROWS - VALID), (0, 0)))
+    def cells_of(v):
+        return jnp.transpose(v, (1, 2, 0, 3)).reshape(CELLS, 2, CH)
 
     def images_of(v):
-        return jnp.transpose(v[:VALID].reshape(14, 14, 2, CH), (2, 0, 1, 3))
+        return jnp.transpose(v.reshape(14, 14, 2, CH), (2, 0, 1, 3))
 
     V = pltpu.VMEM
     n_copies = 130
@@ -461,16 +473,16 @@
     proj, gh, gp = pl.pallas_call(
         kernel,
         out_shape=(
-            jax.ShapeDtypeStruct((ROWS, CH), BF),
-            jax.ShapeDtypeStruct((ROWS, CH), BF),
+            jax.ShapeDtypeStruct((VALID, CH), BF),
+            jax.ShapeDtypeStruct((VALID, CH), BF),
             jax.ShapeDtypeStruct((OWN, CH), F32),
         ),
         in_specs=[any_spec] * 6,
         out_specs=(any_spec,) * 3,
         scratch_shapes=[
-            V((ROWS, CH), BF), V((3, 3, 64, CH), BF), V((CH, SE), BF), V((SE, CH), BF),
+            V((CELLS, 2, CH), BF), V((3, 3, 64, CH), BF), V((CH, SE), BF), V((SE, CH), BF),
             V((9, CH, CH), BF), V((ROWS, CH), F32), V((ROWS, CH), BF),
-            V((NZL, ROWS, CH), BF), V((NX, CH, SLAB), BF), V((2, 64, SLAB), BF),
+            V((NZL, CELLS, 2, CH), BF), V((NZL, ROWS, CH), BF), V((SLAB, ROWS), BF), V((NX, CH, SLAB), BF), V((2, 64, SLAB), BF),
             V((NX, ROWS, CH), BF), V((NX * NZL, 2, SE), F32), V((NX * NZL, 2, SE), F32),
             V((NZL, ROWS, CH), F32), V((NZL, ROWS, CH), BF), V((2, ROWS, CH), BF),
             V((ROWS, CH), F32), V((ROWS, CH), F32), V((3, ROWS, CH), BF),
@@ -486,7 +498,7 @@
             collective_id=0, has_side_effects=True, vmem_limit_bytes=60 * 2**20
         ),
         name="block",
-    )(rows_of(hidden), conv_weight, se_down, se_up, proj_weight, rows_of(grad_out))
+    )(cells_of(hidden), conv_weight, se_down, se_up, proj_weight, cells_of(grad_out))
     return images_of(proj), images_of(gh), gp.T
 
 

time: 76.2 us -> 71.9 us (0.944)
  the two profiles are of different devices: /device:TPU:4 before, /device:TPU:1 now
where the time goes in v2:
time: 71.9 us; the launch traced here: 71.7 us
  Pallas kernels  66.3 us (92%)
  local copies, waits for them, and re-layouts  4.79 us (7%)
    pallas_call x1, Pallas kernels, on_device(): pl.pallas_call(kernel, out_shape=(jax.ShapeDtypeStruct((VALID, CH), BF),...  66.3 us
    reshape x2, local copies, waits for them, and re-layouts, images_of(): return jnp.transpose(v.reshape(14, 14, 2, CH), (2, 0, 1, 3))  3.37 us

profile of v2, /device:TPU:1, one launch (start us, length us, event | category | flops | bytes accessed | tf_op | source)
XLA Modules:
  0.0 71.7 jit_solution(7227570904959499097)
XLA Ops:
  0.6 66.3 %block.1 = (bf16[392,256]{1,0:T(8,128)(2,1)}, bf16[392,256]{1,0:T(8,128)(2,1)}, f32[48,256]{1,0:T(8,128)}) custom-call(bf16[196,2,256]{2,1,0:T(2,128)(2,1)} %bitcast.9, bf16[3,3,64,256]{3,2,1,0:T(8,128)(2,1)} %cw_h.1, bf16[256,1024]{1,0:T(8,128)(2,1)} %down_h.1, bf16[1024,256]{1,0:T(8,128)(2,1)} %up_h.1, bf16[256,3072]{1,0:T(8,128)(2,1)} %w_h.1, ...), custom_call_target="tpu_custom_call" | custom-call | tf_op jit(solution)/shard_map/block/pallas_call | solution.py:473
  66.9 1.7 %reshape.20 = bf16[14,14,2,256]{3,2,1,0:T(2,128)(2,1)} reshape(bf16[392,256]{1,0:T(8,128)(2,1)} %get-tuple-element.6) | data formatting | bytes 401408 | tf_op jit(solution)/shard_map/reshape | solution.py:468
  68.6 1.7 %reshape.21 = bf16[14,14,2,256]{3,2,1,0:T(2,128)(2,1)} reshape(bf16[392,256]{1,0:T(8,128)(2,1)} %get-tuple-element.7) | data formatting | bytes 401408 | tf_op jit(solution)/shard_map/reshape | solution.py:468
  70.3 1.4 %copy.10 = f32[256,48]{0,1:T(8,128)} copy(f32[256,48]{0,1:T(8,128)} %bitcast.13) | data formatting | bytes 98304

commit v3 on v2

--- a/solution.py
+++ b/solution.py
@@ -102,7 +102,7 @@
 def kernel(
     hid_h, cw_h, down_h, up_h, w_h, g_h,
     proj_o, gh_o, gp_o,
-    hid_v, cw_v, down_v, up_v, bd, conv_v, act_v,
+    hid_v, cw_v, down_v, up_v, bd, conv_v, acts, gates,
     graw, gs, gt, wg, wrel, xs, se1, se2,
     p32, psend, precv,
     qown, qnear, qsend, qrel, qdir, qcomb, qcs,
@@ -162,6 +162,8 @@
     greet(dev(core_=core2))
     greet(dev(y_=(y + 1) % NY))
     greet(dev(y_=(y + NY - 1) % NY))
+    greet(dev(y_=(y + 3) % NY))
+    greet(dev(y_=(y + NY - 3) % NY))
     for h in range(NZH):
         greet(dev(x_=zh, zh_=h))
 
@@ -178,12 +180,12 @@
     conv = jnp.where(row < VALID, conv, 0.0)
     conv_v[...] = conv
     act = (conv * sigmoid(conv)).astype(BF)
-    act_v[...] = act
+    acts[x] = act
     squeezed = image_sums(act.astype(F32)) * (1.0 / CELLS)
     loads["down"].wait()
     se1[ch] = join3(dot(split3(squeezed), down_v[...]))
 
-    pl.semaphore_wait(barrier, NX * NZL - 1 + 3 + NZH)
+    pl.semaphore_wait(barrier, NX * NZL - 1 + 5 + NZH)
 
     def se_push(buf):
         out = []
@@ -193,26 +195,24 @@
 
     se_copies = se_push(se1)
 
-    w_rel, w_near = {}, {}
+    w_rel, w_near, w_fwd = {}, {}, {}
     for d in (1, -1):
         at = 0 if d == 1 else 1
         far = pl.multiple_of(xp[2] * SLAB, SLAB)
         w_rel[d] = go(rcopy(
             w_h.at[pl.ds(pl.multiple_of(r0 + 64 * at, 64), 64), pl.ds(far, SLAB)],
             wrel.at[at], dev(x_=xp[d])))
-    def w_near_copy(d, part):
+
+    for d in (1, -1):
         near = pl.multiple_of(xp[d] * SLAB, SLAB)
-        rows = pl.ds(pl.multiple_of(r0 + 64 * part, 64), 64)
-        return go(rcopy(w_h.at[rows, pl.ds(near, SLAB)], wg.at[x, rows, :], dev(x_=xp[d])))
-
-    for d in (1, -1):
-        w_near[d, 0] = w_near_copy(d, 0)
+        w_near[d] = go(rcopy(
+            w_h.at[pl.ds(r0, 128), pl.ds(near, SLAB)],
+            wg.at[x, pl.ds(r0, 128), :], dev(x_=xp[d])))
 
     g_copies = []
     for k in range(1, NZL):
         g_copies.append(go(rcopy(g_h, graw.at[zl], dev(zl_=(zl + k) % NZL))))
 
-    w_fwd = {}
     for d in (1, -1):
         at = 0 if d == 1 else 1
         w_rel[d].wait_recv()
@@ -220,6 +220,14 @@
             wrel.at[at],
             wg.at[xp[-d], pl.ds(pl.multiple_of(r0 + 64 * at, 64), 64), :],
             dev(x_=xp[d])))
+
+    a_first, a_rest, a_fwd = {}, {}, {}
+    for d in (1, -1):
+        ref = acts.at[x, pl.ds(*HALF[d]), :]
+        a_first[d] = go(rcopy(ref, ref, dev(x_=xp[d])))
+    for d in (1, -1):
+        ref = acts.at[x, pl.ds(*HALF[-d]), :]
+        a_rest[d] = go(rcopy(ref, ref, dev(x_=xp[d])))
 
     loads["up"].wait()
     for c in se_copies:
@@ -228,36 +236,22 @@
     for k in range(1, NX * NZL):
         pre = pre + se1[k]
     gating = sigmoid(join3(dot(split3(pre * sigmoid(pre)), up_v[...])))
-    g8 = per_image(gating)
-    xs[x] = scale_rows(act_v[...].astype(F32), g8).astype(BF)
-
-    x_first, x_rest, x_fwd = {}, {}, {}
-    for d in (1, -1):
-        a, n = HALF[d]
-        x_first[d] = go(rcopy(xs.at[x, pl.ds(a, n), :], xs.at[x, pl.ds(a, n), :], dev(x_=xp[d])))
-    for d in (1, -1):
-        a, n = HALF[-d]
-        x_rest[d] = go(rcopy(xs.at[x, pl.ds(a, n), :], xs.at[x, pl.ds(a, n), :], dev(x_=xp[d])))
-
-    for d in (1, -1):
-        a, n = HALF[d]
-        x_first[d].wait_recv()
-        ref = xs.at[xp[-d], pl.ds(a, n), :]
-        x_fwd[d] = go(rcopy(ref, ref, dev(x_=xp[d])))
-    for d in (1, -1):
-        w_near[d, 1] = w_near_copy(d, 1)
+    gates[x] = gating
+    gate_copies = []
+    for k in range(1, NX):
+        gate_copies.append(go(rcopy(gates.at[x], gates.at[x], dev(x_=(x + k) % NX))))
 
     w_sib = []
 
-    def w_share(copy, slot, part):
+    def w_share(copy, slot, first, count):
         copy.wait_recv()
-        ref = wg.at[slot, pl.ds(pl.multiple_of(r0 + 64 * part, 64), 64), :]
+        ref = wg.at[slot, pl.ds(pl.multiple_of(r0 + first, 64), count), :]
         w_sib.append(go(rcopy(ref, ref, dev(core_=core2))))
 
     for d in (1, -1):
-        w_share(w_near[d, 0], xp[-d], 0)
-    for d in (1, -1):
-        w_share(w_fwd[d], xp[2], 0 if d == 1 else 1)
+        w_share(w_near[d], xp[-d], 0, 128)
+    for d in (1, -1):
+        w_share(w_fwd[d], xp[2], 0 if d == 1 else 64, 64)
 
     loads["g"].wait()
     for c in g_copies:
@@ -265,9 +259,19 @@
     for z in range(NZL):
         gs[z] = rows_of(graw[z].astype(F32)).astype(BF)
 
+    for d in (1, -1):
+        a_first[d].wait_recv()
+        ref = acts.at[xp[-d], pl.ds(*HALF[d]), :]
+        a_fwd[d] = go(rcopy(ref, ref, dev(x_=xp[d])))
+
+    subs = (x, xp[-1], xp[1], xp[2])
+    g8 = per_image(gating)
+
+    def scale(xi):
+        xs[xi] = scale_rows(acts[xi].astype(F32), per_image(gates[xi])).astype(BF)
+
     gcat = jnp.concatenate([gs[0], gs[1], gs[2]], axis=1)
     gt[...] = gcat.T
-    subs = (x, xp[-1], xp[1], xp[2])
 
     c_copies = []
 
@@ -276,24 +280,31 @@
         cs[j] = dw[j, :, core2].astype(BF)
         c_copies.append(go(rcopy(cs.at[j], cr.at[j], dev(core_=core2))))
 
-    y_dir = lambda j: -1 if j % 2 == 0 else 1
-    y_last = {}
-
-    def y_step(j, s):
-        for long in (True, False):
-            hops = 4 if long else 3
-            if s > hops:
-                continue
-            e = y_dir(j) if long else -y_dir(j)
-            base = 0 if long else 4
-            owner = (y + e * (hops + 1 - s) + NY) % NY
-            v = dsum[j, owner]
-            if s > 1:
-                y_last[j, long].wait_recv()
-                v = v + yrecv[j, base + s - 2].astype(F32)
-            ysend[j, base + s - 1] = v.astype(BF)
-            y_last[j, long] = go(rcopy(
-                ysend.at[j, base + s - 1], yrecv.at[j, base + s - 1], dev(y_=(y + e + NY) % NY)))
+    y_sent = {}
+
+    def y_of(d):
+        return (y + d + NY) % NY
+
+    def y_first(j):
+        e = 1 if j % 2 else -1
+        ysend[j, 0] = dsum[j, y_of(2 * e)].astype(BF)
+        ysend[j, 1] = dsum[j, y_of(4)].astype(BF)
+        ysend[j, 2] = dsum[j, y_of(-2 * e)].astype(BF)
+        ysend[j, 3] = dsum[j, y_of(-3 * e)].astype(BF)
+        for name, at, n, d in (("near", 0, 2, e), ("back", 2, 1, -e), ("far", 3, 1, -3 * e)):
+            y_sent[j, name] = go(rcopy(
+                ysend.at[j, pl.ds(at, n)], yrecv.at[j, pl.ds(at, n)], dev(y_=y_of(d))))
+
+    def y_second(j):
+        e = 1 if j % 2 else -1
+        y_sent[j, "near"].wait_recv()
+        ysend[j, 4] = (dsum[j, y_of(e)] + yrecv[j, 0].astype(F32)).astype(BF)
+        ysend[j, 5] = (dsum[j, y_of(3 * e)] + yrecv[j, 1].astype(F32)).astype(BF)
+        y_sent[j, "two"] = go(rcopy(ysend.at[j, 5], yrecv.at[j, 5], dev(y_=y_of(3 * e))))
+        y_sent[j, "one"] = go(rcopy(ysend.at[j, 4], yrecv.at[j, 4], dev(y_=y_of(e))))
+        y_sent[j, "back"].wait_recv()
+        ysend[j, 6] = (dsum[j, y_of(-e)] + yrecv[j, 2].astype(F32)).astype(BF)
+        y_sent[j, "last"] = go(rcopy(ysend.at[j, 6], yrecv.at[j, 6], dev(y_=y_of(-e))))
 
     def core_sum(j):
         c_copies[j].wait_recv()
@@ -310,9 +321,11 @@
             device_id=dev(x_=to_x, zh_=x), device_id_type=pl.DeviceIdType.MESH)
 
     def z_push(j):
-        y_last[j, True].wait_recv()
-        y_last[j, False].wait_recv()
-        total = dsum[j, y] + yrecv[j, 3].astype(F32) + yrecv[j, 6].astype(F32)
+        for name in ("far", "one", "two", "last"):
+            y_sent[j, name].wait_recv()
+        total = dsum[j, y]
+        for k in (3, 4, 5, 6):
+            total = total + yrecv[j, k].astype(F32)
         zsend[j] = total.astype(BF)
         if j == 0:
             @pl.when(itself)
@@ -325,27 +338,52 @@
         else:
             go(z_copy(j, subs[j]))
 
+    scale(x)
     weight_grad(0)
-    x_rest[1].wait_recv()
-    weight_grad(1)
-    core_sum(0)
-    y_step(0, 1)
-    x_rest[-1].wait_recv()
-    weight_grad(2)
-    for d in (1, -1):
-        x_fwd[d].wait_recv()
-    weight_grad(3)
-    for j in (1, 2):
-        core_sum(j)
-        y_step(j, 1)
-    y_step(0, 2)
 
     loads["w"].wait()
-    xcat = jnp.concatenate([xs[0], xs[1], xs[2], xs[3]], axis=1)
-    for d in (1, -1):
-        w_share(w_near[d, 1], xp[-d], 1)
     for c in w_sib:
         c.wait_recv()
+
+    def q_part(xi):
+        return dot_nt(gcat, wg[xi])
+
+    q_rel, q_dir, q_comb = {}, {}, {}
+    qsend[0] = q_part(xp[2]).astype(BF)
+    for d in (1, -1):
+        a, n = HALF[d]
+        q_rel[d] = go(rcopy(
+            qsend.at[0, pl.ds(a, n), :], qrel.at[pl.ds(a, n), :], dev(x_=xp[d])))
+    for d in (1, -1):
+        at = 0 if d == 1 else 1
+        a, n = HALF[d]
+        b, m = HALF[-d]
+        part = q_part(xp[d])
+        qsend[1 + at] = part.astype(BF)
+        qnear[pl.ds(a, n), :] = part[a:a + n]
+        q_dir[d] = go(rcopy(
+            qsend.at[1 + at, pl.ds(b, m), :], qdir.at[pl.ds(b, m), :], dev(x_=xp[d])))
+    qown[...] = q_part(x)
+
+    core_sum(0)
+    y_first(0)
+
+    for c in gate_copies:
+        c.wait_recv()
+    for j, d in ((1, 1), (2, -1)):
+        a_rest[d].wait_recv()
+    for d in (1, -1):
+        scale(xp[-d])
+    weight_grad(1)
+    weight_grad(2)
+    for d in (1, -1):
+        a_fwd[d].wait_recv()
+    scale(xp[2])
+    weight_grad(3)
+    core_sum(1)
+    y_first(1)
+
+    xcat = jnp.concatenate([xs[0], xs[1], xs[2], xs[3]], axis=1)
     wcat = wg[...].reshape(NX * CH, SLAB)
     for zo in range(NZL):
         part = dot(xcat, wcat[:, zo * CH:(zo + 1) * CH])
@@ -355,36 +393,10 @@
     for k in range(1, NZL):
         p_copies.append(go(rcopy(
             psend.at[(zl + k) % NZL], precv.at[k - 1], dev(zl_=(zl + k) % NZL))))
-    def q_part(xi):
-        return dot_nt(gcat, wg[xi])
-
-    q_rel, q_dir, q_comb = {}, {}, {}
-    qsend[0] = q_part(xp[2]).astype(BF)
-    for d in (1, -1):
-        a, n = HALF[d]
-        q_rel[d] = go(rcopy(
-            qsend.at[0, pl.ds(a, n), :], qrel.at[pl.ds(a, n), :], dev(x_=xp[d])))
-    for d in (1, -1):
-        at = 0 if d == 1 else 1
-        a, n = HALF[d]
-        b, m = HALF[-d]
-        part = q_part(xp[d])
-        qsend[1 + at] = part.astype(BF)
-        qnear[pl.ds(a, n), :] = part[a:a + n]
-        q_dir[d] = go(rcopy(
-            qsend.at[1 + at, pl.ds(b, m), :], qdir.at[pl.ds(b, m), :], dev(x_=xp[d])))
-    qown[...] = q_part(x)
-    core_sum(3)
-    y_step(3, 1)
-    y_step(1, 2)
-    y_step(2, 2)
-    y_step(0, 3)
-    y_step(3, 2)
-    y_step(0, 4)
-    y_step(1, 3)
-    y_step(2, 3)
-    y_step(3, 3)
-    z_push(0)
+
+    for j in (2, 3):
+        core_sum(j)
+        y_first(j)
     for d in (1, -1):
         a, n = HALF[d]
         q_rel[d].wait_recv()
@@ -392,21 +404,21 @@
         q_comb[d] = go(rcopy(
             qcs.at[pl.ds(a, n), :], qcomb.at[pl.ds(a, n), :], dev(x_=xp[d])))
 
-    y_step(1, 4)
-    y_step(2, 4)
-    y_step(3, 4)
+    for j in range(4):
+        y_second(j)
+    z_push(0)
     z_push(1)
-    z_push(2)
-    z_push(3)
+
     for d in (1, -1):
         q_dir[d].wait_recv()
         q_comb[d].wait_recv()
     qown[...] = qown[...] + qdir[...].astype(F32) + qcomb[...].astype(F32)
-    gate_grad = image_sums(qown[...] * act_v[...].astype(F32))
+    gate_grad = image_sums(qown[...] * acts[x].astype(F32))
     pre_grad = gate_grad * gating * (1.0 - gating)
     se2[ch] = join3(dot_nt(split3(pre_grad), up_v[...]))
     se_copies = se_push(se2)
-
+    z_push(2)
+    z_push(3)
 
     for c in p_copies:
         c.wait_recv()
@@ -481,7 +493,7 @@
         out_specs=(any_spec,) * 3,
         scratch_shapes=[
             V((CELLS, 2, CH), BF), V((3, 3, 64, CH), BF), V((CH, SE), BF), V((SE, CH), BF),
-            V((9, CH, CH), BF), V((ROWS, CH), F32), V((ROWS, CH), BF),
+            V((9, CH, CH), BF), V((ROWS, CH), F32), V((NX, ROWS, CH), BF), V((NX, 2, CH), F32),
             V((NZL, CELLS, 2, CH), BF), V((NZL, ROWS, CH), BF), V((SLAB, ROWS), BF), V((NX, CH, SLAB), BF), V((2, 64, SLAB), BF),
             V((NX, ROWS, CH), BF), V((NX * NZL, 2, SE), F32), V((NX * NZL, 2, SE), F32),
             V((NZL, ROWS, CH), F32), V((NZL, ROWS, CH), BF), V((2, ROWS, CH), BF),

time: 71.9 us -> 69.1 us (0.961)
  the two profiles are of different devices: /device:TPU:1 before, /device:TPU:10 now
where the time goes in v3:
time: 69.1 us; the launch traced here: 68.9 us
  Pallas kernels  63.4 us (92%)
  local copies, waits for them, and re-layouts  4.79 us (7%)
    pallas_call x1, Pallas kernels, on_device(): pl.pallas_call(kernel, out_shape=(jax.ShapeDtypeStruct((VALID, CH), BF),...  63.4 us
    reshape x2, local copies, waits for them, and re-layouts, images_of(): return jnp.transpose(v.reshape(14, 14, 2, CH), (2, 0, 1, 3))  3.37 us
    unnamed x1, local copies, waits for them, and re-layouts  1.42 us

profile of v3, /device:TPU:10, one launch (start us, length us, event | category | flops | bytes accessed | tf_op | source)
XLA Modules:
  0.0 68.9 jit_solution(14510214472125800879)
XLA Ops:
  0.6 63.4 %block.1 = (bf16[392,256]{1,0:T(8,128)(2,1)}, bf16[392,256]{1,0:T(8,128)(2,1)}, f32[48,256]{1,0:T(8,128)}) custom-call(bf16[196,2,256]{2,1,0:T(2,128)(2,1)} %bitcast.9, bf16[3,3,64,256]{3,2,1,0:T(8,128)(2,1)} %cw_h.1, bf16[256,1024]{1,0:T(8,128)(2,1)} %down_h.1, bf16[1024,256]{1,0:T(8,128)(2,1)} %up_h.1, bf16[256,3072]{1,0:T(8,128)(2,1)} %w_h.1, ...), custom_call_target="tpu_custom_call" | custom-call | tf_op jit(solution)/shard_map/block/pallas_call | solution.py:485
  64.1 1.7 %reshape.20 = bf16[14,14,2,256]{3,2,1,0:T(2,128)(2,1)} reshape(bf16[392,256]{1,0:T(8,128)(2,1)} %get-tuple-element.6) | data formatting | bytes 401408 | tf_op jit(solution)/shard_map/reshape | solution.py:480
  65.8 1.7 %reshape.21 = bf16[14,14,2,256]{3,2,1,0:T(2,128)(2,1)} reshape(bf16[392,256]{1,0:T(8,128)(2,1)} %get-tuple-element.7) | data formatting | bytes 401408 | tf_op jit(solution)/shard_map/reshape | solution.py:480
  67.4 1.4 %copy.10 = f32[256,48]{0,1:T(8,128)} copy(f32[256,48]{0,1:T(8,128)} %bitcast.13) | data formatting | bytes 98304

commit v4 on v3

--- a/solution.py
+++ b/solution.py
@@ -17,16 +17,6 @@
 SE = 1024
 OWN = 48
 HALF = {1: (0, 208), -1: (208, 192)}
-
-
-class Sems:
-    def __init__(self, send, recv):
-        self.send, self.recv, self.n_send, self.n_recv = send, recv, 0, 0
-
-    def take(self, count=1):
-        at = self.n_send
-        self.n_send += count
-        return at
 
 
 def dot(a, b):
@@ -107,8 +97,7 @@
     p32, psend, precv,
     qown, qnear, qsend, qrel, qdir, qcomb, qcs,
     dw, cs, cr, dsum, ysend, yrecv, zsend, zrecv,
-    proj_v, gh_v, gp_v,
-    lsem, osem, ssem, rsem,
+    lsem, ssem, rsem,
 ):
     dp = lax.axis_index("dp")
     ch = lax.axis_index("chan")
@@ -124,7 +113,7 @@
     counter = [0]
     sends = []
 
-    def rcopy(src, dst, to, key=None):
+    def rcopy(src, dst, to):
         i = counter[0]
         counter[0] += 1
         c = pltpu.make_async_remote_copy(
@@ -142,6 +131,21 @@
     core2 = 1 - core
     slab0 = pl.multiple_of(x * SLAB, SLAB)
     r0 = pl.multiple_of(core * 128, 128)
+
+    barrier = pltpu.get_barrier_semaphore()
+
+    def greet(to):
+        pl.semaphore_signal(barrier, inc=1, device_id=to, device_id_type=pl.DeviceIdType.MESH)
+
+    for h in range(NZH):
+        greet(dev(x_=zh, zh_=h))
+    for k in range(1, NX * NZL):
+        greet({"dp": dp, "chan": (ch + k) % (NX * NZL)})
+    greet(dev(core_=core2))
+    greet(dev(y_=(y + 1) % NY))
+    greet(dev(y_=(y + NY - 1) % NY))
+    greet(dev(y_=(y + 3) % NY))
+    greet(dev(y_=(y + NY - 3) % NY))
 
     loads = {}
     for i, (name, src, dst) in enumerate((
@@ -151,21 +155,6 @@
     )):
         loads[name] = pltpu.make_async_copy(src, dst, lsem.at[i])
         loads[name].start()
-
-    barrier = pltpu.get_barrier_semaphore()
-
-    def greet(to):
-        pl.semaphore_signal(barrier, inc=1, device_id=to, device_id_type=pl.DeviceIdType.MESH)
-
-    for k in range(1, NX * NZL):
-        greet({"dp": dp, "chan": (ch + k) % (NX * NZL)})
-    greet(dev(core_=core2))
-    greet(dev(y_=(y + 1) % NY))
-    greet(dev(y_=(y + NY - 1) % NY))
-    greet(dev(y_=(y + 3) % NY))
-    greet(dev(y_=(y + NY - 3) % NY))
-    for h in range(NZH):
-        greet(dev(x_=zh, zh_=h))
 
     loads["hid"].wait()
     loads["cw"].wait()
@@ -380,8 +369,9 @@
         a_fwd[d].wait_recv()
     scale(xp[2])
     weight_grad(3)
-    core_sum(1)
-    y_first(1)
+    for j in (1, 2):
+        core_sum(j)
+        y_first(j)
 
     xcat = jnp.concatenate([xs[0], xs[1], xs[2], xs[3]], axis=1)
     wcat = wg[...].reshape(NX * CH, SLAB)
@@ -394,9 +384,9 @@
         p_copies.append(go(rcopy(
             psend.at[(zl + k) % NZL], precv.at[k - 1], dev(zl_=(zl + k) % NZL))))
 
-    for j in (2, 3):
-        core_sum(j)
-        y_first(j)
+    core_sum(3)
+    y_first(3)
+    y_second(0)
     for d in (1, -1):
         a, n = HALF[d]
         q_rel[d].wait_recv()
@@ -404,7 +394,7 @@
         q_comb[d] = go(rcopy(
             qcs.at[pl.ds(a, n), :], qcomb.at[pl.ds(a, n), :], dev(x_=xp[d])))
 
-    for j in range(4):
+    for j in range(1, 4):
         y_second(j)
     z_push(0)
     z_push(1)
@@ -423,9 +413,7 @@
     for c in p_copies:
         c.wait_recv()
     proj = p32[zl] + precv[0].astype(F32) + precv[1].astype(F32)
-    proj_v[...] = proj.astype(BF)
-    proj_copy = pltpu.make_async_copy(proj_v.at[pl.ds(0, VALID), :], proj_o, osem.at[1])
-    proj_copy.start()
+    proj_o[...] = proj[:VALID].astype(BF)
 
     for c in se_copies:
         c.wait_recv()
@@ -441,9 +429,7 @@
     conv_grad = act_grad.reshape(ROWS, CH) * silu_grad(conv_v[...])
     conv_grad = conv_grad.astype(BF).astype(F32)
     turned = jnp.concatenate([bd[8 - t] for t in range(9)], axis=1)
-    gh_v[...] = dot_nt(taps(conv_grad), turned).astype(BF)
-    gh_copy = pltpu.make_async_copy(gh_v.at[pl.ds(0, VALID), :], gh_o, osem.at[0])
-    gh_copy.start()
+    gh_o[...] = dot_nt(taps(conv_grad), turned)[:VALID].astype(BF)
 
     for h in range(NZH):
         @pl.when(jnp.logical_not(jnp.logical_and(itself, zh == h)))
@@ -456,9 +442,7 @@
     gp = zrecv[0].astype(F32)
     for h in range(1, NZH):
         gp = gp + zrecv[h].astype(F32)
-    gp_v[...] = gp
-    gp_copy = pltpu.make_async_copy(gp_v, gp_o, osem.at[2])
-    gp_copy.start()
+    gp_o[...] = gp
 
     for c in sends:
         c.wait_send()
@@ -466,10 +450,6 @@
     @pl.when(jnp.logical_not(itself))
     def _():
         z_copy(0, subs[0]).wait_send()
-
-    gh_copy.wait()
-    proj_copy.wait()
-    gp_copy.wait()
 
 
 def on_device(hidden, conv_weight, se_down, se_up, proj_weight, grad_out):
@@ -484,13 +464,9 @@
     any_spec = pl.BlockSpec(memory_space=pl.ANY)
     proj, gh, gp = pl.pallas_call(
         kernel,
-        out_shape=(
-            jax.ShapeDtypeStruct((VALID, CH), BF),
-            jax.ShapeDtypeStruct((VALID, CH), BF),
-            jax.ShapeDtypeStruct((OWN, CH), F32),
-        ),
+        out_shape=(V((VALID, CH), BF), V((VALID, CH), BF), V((OWN, CH), F32)),
         in_specs=[any_spec] * 6,
-        out_specs=(any_spec,) * 3,
+        out_specs=(pl.BlockSpec(memory_space=pltpu.VMEM),) * 3,
         scratch_shapes=[
             V((CELLS, 2, CH), BF), V((3, 3, 64, CH), BF), V((CH, SE), BF), V((SE, CH), BF),
             V((9, CH, CH), BF), V((ROWS, CH), F32), V((NX, ROWS, CH), BF), V((NX, 2, CH), F32),
@@ -502,15 +478,14 @@
             V((4, NY, NC, OWN, CH), F32), V((4, NY, OWN, CH), BF), V((4, NY, OWN, CH), BF),
             V((4, NY, OWN, CH), F32), V((4, 7, OWN, CH), BF), V((4, 7, OWN, CH), BF),
             V((4, OWN, CH), BF), V((NZH, OWN, CH), BF),
-            V((ROWS, CH), BF), V((ROWS, CH), BF), V((OWN, CH), F32),
-            pltpu.SemaphoreType.DMA((6,)), pltpu.SemaphoreType.DMA((3,)),
+            pltpu.SemaphoreType.DMA((6,)),
             pltpu.SemaphoreType.DMA((n_copies,)), pltpu.SemaphoreType.DMA((n_copies,)),
         ],
         compiler_params=pltpu.CompilerParams(
-            collective_id=0, has_side_effects=True, vmem_limit_bytes=60 * 2**20
+            collective_id=0, has_side_effects=True, vmem_limit_bytes=40 * 2**20
         ),
         name="block",
-    )(cells_of(hidden), conv_weight, se_down, se_up, proj_weight, cells_of(grad_out))
+    )(*[pltpu.with_memory_space_constraint(v, pltpu.HBM) for v in (cells_of(hidden), conv_weight, se_down, se_up, proj_weight, cells_of(grad_out))])
     return images_of(proj), images_of(gh), gp.T
 
 

time: 69.1 us -> 65.3 us (0.945)
  the two profiles are of different devices: /device:TPU:10 before, /device:TPU:24 now
where the time goes in v4:
time: 65.3 us; the launch traced here: 65.2 us
  Pallas kernels  62.4 us (96%)
  local copies, waits for them, and re-layouts  2.14 us (3%)
    pallas_call x1, Pallas kernels, on_device(): pl.pallas_call(kernel, out_shape=(V((VALID, CH), BF), V((VALID, CH), BF),...  62.4 us
    reshape x2, local copies, waits for them, and re-layouts, images_of(): return jnp.transpose(v.reshape(14, 14, 2, CH), (2, 0, 1, 3))  1.52 us

profile of v4, /device:TPU:24, one launch (start us, length us, event | category | flops | bytes accessed | tf_op | source)
XLA Modules:
  0.0 65.2 jit_solution(7652495568033550374)
XLA Ops:
  0.6 62.4 %block.1 = (bf16[392,256]{1,0:T(8,128)(2,1)S(1)}, bf16[392,256]{1,0:T(8,128)(2,1)S(1)}, f32[48,256]{1,0:T(8,128)S(1)}) custom-call(bf16[196,2,256]{2,1,0:T(2,128)(2,1)} %bitcast.10, bf16[3,3,64,256]{3,2,1,0:T(8,128)(2,1)} %cw_h.1, bf16[256,1024]{1,0:T(8,128)(2,1)} %down_h.1, bf16[1024,256]{1,0:T(8,128)(2,1)} %up_h.1, bf16[256,3072]{1,0:T(8,128)(2,1)} %w_h.1, ...), custom_call_target="tpu_custom_call" | custom-call | tf_op jit(solution)/shard_map/block/pallas_call | solution.py:465
  63.0 0.8 %reshape.20 = bf16[14,14,2,256]{3,2,1,0:T(2,128)(2,1)} reshape(bf16[392,256]{1,0:T(8,128)(2,1)S(1)} %get-tuple-element.6) | data formatting | bytes 401408 | tf_op jit(solution)/shard_map/reshape | solution.py:460
  63.8 0.6 copy.10
  64.4 0.8 %reshape.21 = bf16[14,14,2,256]{3,2,1,0:T(2,128)(2,1)} reshape(bf16[392,256]{1,0:T(8,128)(2,1)S(1)} %get-tuple-element.7) | data formatting | bytes 401408 | tf_op jit(solution)/shard_map/reshape | solution.py:460

commit v5 on v4

--- a/solution.py
+++ b/solution.py
@@ -130,7 +130,8 @@
     xp = {1: (x + 1) % NX, -1: (x + NX - 1) % NX, 2: (x + 2) % NX}
     core2 = 1 - core
     slab0 = pl.multiple_of(x * SLAB, SLAB)
-    r0 = pl.multiple_of(core * 128, 128)
+    pair = y + 1 - 2 * (y % 2)
+    r0 = pl.multiple_of((y % 2) * 128 + core * 64, 64)
 
     barrier = pltpu.get_barrier_semaphore()
 
@@ -189,14 +190,14 @@
         at = 0 if d == 1 else 1
         far = pl.multiple_of(xp[2] * SLAB, SLAB)
         w_rel[d] = go(rcopy(
-            w_h.at[pl.ds(pl.multiple_of(r0 + 64 * at, 64), 64), pl.ds(far, SLAB)],
+            w_h.at[pl.ds(pl.multiple_of(r0 + 32 * at, 32), 32), pl.ds(far, SLAB)],
             wrel.at[at], dev(x_=xp[d])))
 
     for d in (1, -1):
         near = pl.multiple_of(xp[d] * SLAB, SLAB)
         w_near[d] = go(rcopy(
-            w_h.at[pl.ds(r0, 128), pl.ds(near, SLAB)],
-            wg.at[x, pl.ds(r0, 128), :], dev(x_=xp[d])))
+            w_h.at[pl.ds(r0, 64), pl.ds(near, SLAB)],
+            wg.at[x, pl.ds(r0, 64), :], dev(x_=xp[d])))
 
     g_copies = []
     for k in range(1, NZL):
@@ -207,7 +208,7 @@
         w_rel[d].wait_recv()
         w_fwd[d] = go(rcopy(
             wrel.at[at],
-            wg.at[xp[-d], pl.ds(pl.multiple_of(r0 + 64 * at, 64), 64), :],
+            wg.at[xp[-d], pl.ds(pl.multiple_of(r0 + 32 * at, 32), 32), :],
             dev(x_=xp[d])))
 
     a_first, a_rest, a_fwd = {}, {}, {}
@@ -230,28 +231,39 @@
     for k in range(1, NX):
         gate_copies.append(go(rcopy(gates.at[x], gates.at[x], dev(x_=(x + k) % NX))))
 
-    w_sib = []
+    w_sib, w_pair = [], []
 
     def w_share(copy, slot, first, count):
         copy.wait_recv()
-        ref = wg.at[slot, pl.ds(pl.multiple_of(r0 + first, 64), count), :]
+        ref = wg.at[slot, pl.ds(pl.multiple_of(r0 + first, 32), count), :]
+        w_pair.append((go(rcopy(ref, ref, dev(y_=pair))), slot, first, count))
         w_sib.append(go(rcopy(ref, ref, dev(core_=core2))))
 
-    for d in (1, -1):
-        w_share(w_near[d], xp[-d], 0, 128)
-    for d in (1, -1):
-        w_share(w_fwd[d], xp[2], 0 if d == 1 else 64, 64)
+    def w_pass(k):
+        copy, slot, first, count = w_pair[k]
+        copy.wait_recv()
+        r1 = (1 - y % 2) * 128 + core * 64
+        ref = wg.at[slot, pl.ds(pl.multiple_of(r1 + first, 32), count), :]
+        w_sib.append(go(rcopy(ref, ref, dev(core_=core2))))
+
+    for d in (1, -1):
+        w_share(w_near[d], xp[-d], 0, 64)
+    for d in (1, -1):
+        w_share(w_fwd[d], xp[2], 0 if d == 1 else 32, 32)
+
+    for d in (1, -1):
+        a_first[d].wait_recv()
+        ref = acts.at[xp[-d], pl.ds(*HALF[d]), :]
+        a_fwd[d] = go(rcopy(ref, ref, dev(x_=xp[d])))
+
+    w_pass(0)
+    w_pass(1)
 
     loads["g"].wait()
     for c in g_copies:
         c.wait_recv()
     for z in range(NZL):
         gs[z] = rows_of(graw[z].astype(F32)).astype(BF)
-
-    for d in (1, -1):
-        a_first[d].wait_recv()
-        ref = acts.at[xp[-d], pl.ds(*HALF[d]), :]
-        a_fwd[d] = go(rcopy(ref, ref, dev(x_=xp[d])))
 
     subs = (x, xp[-1], xp[1], xp[2])
     g8 = per_image(gating)
@@ -329,6 +341,23 @@
 
     scale(x)
     weight_grad(0)
+    for c in gate_copies:
+        c.wait_recv()
+    for j, d in ((1, 1), (2, -1)):
+        a_rest[d].wait_recv()
+    for d in (1, -1):
+        scale(xp[-d])
+    weight_grad(1)
+    weight_grad(2)
+    for d in (1, -1):
+        a_fwd[d].wait_recv()
+    scale(xp[2])
+    weight_grad(3)
+    w_pass(2)
+    w_pass(3)
+    for j in range(4):
+        core_sum(j)
+        y_first(j)
 
     loads["w"].wait()
     for c in w_sib:
@@ -353,25 +382,6 @@
         q_dir[d] = go(rcopy(
             qsend.at[1 + at, pl.ds(b, m), :], qdir.at[pl.ds(b, m), :], dev(x_=xp[d])))
     qown[...] = q_part(x)
-
-    core_sum(0)
-    y_first(0)
-
-    for c in gate_copies:
-        c.wait_recv()
-    for j, d in ((1, 1), (2, -1)):
-        a_rest[d].wait_recv()
-    for d in (1, -1):
-        scale(xp[-d])
-    weight_grad(1)
-    weight_grad(2)
-    for d in (1, -1):
-        a_fwd[d].wait_recv()
-    scale(xp[2])
-    weight_grad(3)
-    for j in (1, 2):
-        core_sum(j)
-        y_first(j)
 
     xcat = jnp.concatenate([xs[0], xs[1], xs[2], xs[3]], axis=1)
     wcat = wg[...].reshape(NX * CH, SLAB)
@@ -384,8 +394,6 @@
         p_copies.append(go(rcopy(
             psend.at[(zl + k) % NZL], precv.at[k - 1], dev(zl_=(zl + k) % NZL))))
 
-    core_sum(3)
-    y_first(3)
     y_second(0)
     for d in (1, -1):
         a, n = HALF[d]
@@ -470,7 +478,7 @@
         scratch_shapes=[
             V((CELLS, 2, CH), BF), V((3, 3, 64, CH), BF), V((CH, SE), BF), V((SE, CH), BF),
             V((9, CH, CH), BF), V((ROWS, CH), F32), V((NX, ROWS, CH), BF), V((NX, 2, CH), F32),
-            V((NZL, CELLS, 2, CH), BF), V((NZL, ROWS, CH), BF), V((SLAB, ROWS), BF), V((NX, CH, SLAB), BF), V((2, 64, SLAB), BF),
+            V((NZL, CELLS, 2, CH), BF), V((NZL, ROWS, CH), BF), V((SLAB, ROWS), BF), V((NX, CH, SLAB), BF), V((2, 32, SLAB), BF),
             V((NX, ROWS, CH), BF), V((NX * NZL, 2, SE), F32), V((NX * NZL, 2, SE), F32),
             V((NZL, ROWS, CH), F32), V((NZL, ROWS, CH), BF), V((2, ROWS, CH), BF),
             V((ROWS, CH), F32), V((ROWS, CH), F32), V((3, ROWS, CH), BF),

time: 65.3 us -> 63.4 us (0.971)
  the two profiles are of different devices: /device:TPU:24 before, /device:TPU:69 now
where the time goes in v5:
time: 63.4 us; the launch traced here: 63.2 us
  Pallas kernels  60.5 us (95%)
  local copies, waits for them, and re-layouts  2.14 us (3%)
  between operations  0.64 us (1%)
    pallas_call x1, Pallas kernels, on_device(): pl.pallas_call(kernel, out_shape=(V((VALID, CH), BF), V((VALID, CH), BF),...  60.5 us
    reshape x2, local copies, waits for them, and re-layouts, images_of(): return jnp.transpose(v.reshape(14, 14, 2, CH), (2, 0, 1, 3))  1.52 us

profile of v5, /device:TPU:69, one launch (start us, length us, event | category | flops | bytes accessed | tf_op | source)
XLA Modules:
  0.0 63.2 jit_solution(2488765210944395469)
XLA Ops:
  0.6 60.5 %block.1 = (bf16[392,256]{1,0:T(8,128)(2,1)S(1)}, bf16[392,256]{1,0:T(8,128)(2,1)S(1)}, f32[48,256]{1,0:T(8,128)S(1)}) custom-call(bf16[196,2,256]{2,1,0:T(2,128)(2,1)} %bitcast.10, bf16[3,3,64,256]{3,2,1,0:T(8,128)(2,1)} %cw_h.1, bf16[256,1024]{1,0:T(8,128)(2,1)} %down_h.1, bf16[1024,256]{1,0:T(8,128)(2,1)} %up_h.1, bf16[256,3072]{1,0:T(8,128)(2,1)} %w_h.1, ...), custom_call_target="tpu_custom_call" | custom-call | tf_op jit(solution)/shard_map/block/pallas_call | solution.py:473
  61.1 0.8 %reshape.20 = bf16[14,14,2,256]{3,2,1,0:T(2,128)(2,1)} reshape(bf16[392,256]{1,0:T(8,128)(2,1)S(1)} %get-tuple-element.6) | data formatting | bytes 401408 | tf_op jit(solution)/shard_map/reshape | solution.py:468
  61.9 0.6 copy.10
  62.5 0.8 %reshape.21 = bf16[14,14,2,256]{3,2,1,0:T(2,128)(2,1)} reshape(bf16[392,256]{1,0:T(8,128)(2,1)S(1)} %get-tuple-element.7) | data formatting | bytes 401408 | tf_op jit(solution)/shard_map/reshape | solution.py:468

commit v6 on v5

--- a/solution.py
+++ b/solution.py
@@ -227,9 +227,18 @@
         pre = pre + se1[k]
     gating = sigmoid(join3(dot(split3(pre * sigmoid(pre)), up_v[...])))
     gates[x] = gating
+
+    def take_cotangents(z):
+        block = rows_of(graw[z].astype(F32)).astype(BF)
+        gs[z] = block
+        gt[z] = block.T
+
     gate_copies = []
     for k in range(1, NX):
         gate_copies.append(go(rcopy(gates.at[x], gates.at[x], dev(x_=(x + k) % NX))))
+
+    loads["g"].wait()
+    take_cotangents(zl)
 
     w_sib, w_pair = [], []
 
@@ -259,11 +268,9 @@
     w_pass(0)
     w_pass(1)
 
-    loads["g"].wait()
-    for c in g_copies:
-        c.wait_recv()
-    for z in range(NZL):
-        gs[z] = rows_of(graw[z].astype(F32)).astype(BF)
+    for k in range(1, NZL):
+        g_copies[k - 1].wait_recv()
+        take_cotangents((zl + NZL - k) % NZL)
 
     subs = (x, xp[-1], xp[1], xp[2])
     g8 = per_image(gating)
@@ -272,12 +279,11 @@
         xs[xi] = scale_rows(acts[xi].astype(F32), per_image(gates[xi])).astype(BF)
 
     gcat = jnp.concatenate([gs[0], gs[1], gs[2]], axis=1)
-    gt[...] = gcat.T
 
     c_copies = []
 
     def weight_grad(j):
-        dw[j] = dot(gt[...], xs[subs[j]]).reshape(NY, NC, OWN, CH)
+        dw[j] = dot(gt[...].reshape(SLAB, ROWS), xs[subs[j]]).reshape(NY, NC, OWN, CH)
         cs[j] = dw[j, :, core2].astype(BF)
         c_copies.append(go(rcopy(cs.at[j], cr.at[j], dev(core_=core2))))
 
@@ -421,7 +427,7 @@
     for c in p_copies:
         c.wait_recv()
     proj = p32[zl] + precv[0].astype(F32) + precv[1].astype(F32)
-    proj_o[...] = proj[:VALID].astype(BF)
+    proj_o[...] = proj[:VALID].reshape(CELLS, 2, CH).astype(BF)
 
     for c in se_copies:
         c.wait_recv()
@@ -437,7 +443,7 @@
     conv_grad = act_grad.reshape(ROWS, CH) * silu_grad(conv_v[...])
     conv_grad = conv_grad.astype(BF).astype(F32)
     turned = jnp.concatenate([bd[8 - t] for t in range(9)], axis=1)
-    gh_o[...] = dot_nt(taps(conv_grad), turned)[:VALID].astype(BF)
+    gh_o[...] = dot_nt(taps(conv_grad), turned)[:VALID].reshape(CELLS, 2, CH).astype(BF)
 
     for h in range(NZH):
         @pl.when(jnp.logical_not(jnp.logical_and(itself, zh == h)))
@@ -472,13 +478,13 @@
     any_spec = pl.BlockSpec(memory_space=pl.ANY)
     proj, gh, gp = pl.pallas_call(
         kernel,
-        out_shape=(V((VALID, CH), BF), V((VALID, CH), BF), V((OWN, CH), F32)),
+        out_shape=(V((CELLS, 2, CH), BF), V((CELLS, 2, CH), BF), V((OWN, CH), F32)),
         in_specs=[any_spec] * 6,
         out_specs=(pl.BlockSpec(memory_space=pltpu.VMEM),) * 3,
         scratch_shapes=[
             V((CELLS, 2, CH), BF), V((3, 3, 64, CH), BF), V((CH, SE), BF), V((SE, CH), BF),
             V((9, CH, CH), BF), V((ROWS, CH), F32), V((NX, ROWS, CH), BF), V((NX, 2, CH), F32),
-            V((NZL, CELLS, 2, CH), BF), V((NZL, ROWS, CH), BF), V((SLAB, ROWS), BF), V((NX, CH, SLAB), BF), V((2, 32, SLAB), BF),
+            V((NZL, CELLS, 2, CH), BF), V((NZL, ROWS, CH), BF), V((NZL, CH, ROWS), BF), V((NX, CH, SLAB), BF), V((2, 32, SLAB), BF),
             V((NX, ROWS, CH), BF), V((NX * NZL, 2, SE), F32), V((NX * NZL, 2, SE), F32),
             V((NZL, ROWS, CH), F32), V((NZL, ROWS, CH), BF), V((2, ROWS, CH), BF),
             V((ROWS, CH), F32), V((ROWS, CH), F32), V((3, ROWS, CH), BF),

time: 63.4 us -> 63.4 us (level)
    reshape x2 -> x0, local copies, waits for them, and re-layouts: 1.52 us -> none  [images_of(): return jnp.transpose(v.reshape(14, 14, 2, CH), (2, 0, 1, 3))]
    unnamed x1 -> x3, local copies, waits for them, and re-layouts: 0.62 us -> 1.98 us
where the time goes in v6:
time: 63.4 us; the launch traced here: 63.3 us
  Pallas kernels  60.7 us (96%)
  local copies, waits for them, and re-layouts  1.98 us (3%)
  between operations  0.64 us (1%)
    pallas_call x1, Pallas kernels, on_device(): pl.pallas_call(kernel, out_shape=(V((CELLS, 2, CH), BF), V((CELLS, 2, CH)...  60.7 us
    unnamed x3, local copies, waits for them, and re-layouts  1.98 us

profile of v6, /device:TPU:69, one launch (start us, length us, event | category | flops | bytes accessed | tf_op | source)
XLA Modules:
  0.0 63.3 jit_solution(17804350683117807460)
XLA Ops:
  0.6 60.7 %block.1 = (bf16[196,2,256]{2,1,0:T(2,128)(2,1)S(1)}, bf16[196,2,256]{2,1,0:T(2,128)(2,1)S(1)}, f32[48,256]{1,0:T(8,128)S(1)}) custom-call(bf16[196,2,256]{2,1,0:T(2,128)(2,1)} %bitcast.16, bf16[3,3,64,256]{3,2,1,0:T(8,128)(2,1)} %cw_h.1, bf16[256,1024]{1,0:T(8,128)(2,1)} %down_h.1, bf16[1024,256]{1,0:T(8,128)(2,1)} %up_h.1, bf16[256,3072]{1,0:T(8,128)(2,1)} %w_h.1, ...), custom_call_target="tpu_custom_call" | custom-call | tf_op jit(solution)/shard_map/block/pallas_call | solution.py:479
  61.3 0.7 %copy.12 = bf16[2,14,14,256]{3,0,2,1:T(2,128)(2,1)} copy(bf16[2,14,14,256]{3,0,2,1:T(2,128)(2,1)S(1)} %bitcast.14) | data formatting | bytes 401408
  62.0 0.7 %copy.13 = bf16[2,14,14,256]{3,0,2,1:T(2,128)(2,1)} copy(bf16[2,14,14,256]{3,0,2,1:T(2,128)(2,1)S(1)} %bitcast.13) | data formatting | bytes 401408
  62.7 0.6 copy.14

commit v7 on v6

--- a/solution.py
+++ b/solution.py
@@ -410,8 +410,8 @@
 
     for j in range(1, 4):
         y_second(j)
-    z_push(0)
-    z_push(1)
+    for j in range(4):
+        z_push(j)
 
     for d in (1, -1):
         q_dir[d].wait_recv()
@@ -421,8 +421,6 @@
     pre_grad = gate_grad * gating * (1.0 - gating)
     se2[ch] = join3(dot_nt(split3(pre_grad), up_v[...]))
     se_copies = se_push(se2)
-    z_push(2)
-    z_push(3)
 
     for c in p_copies:
         c.wait_recv()

time: 63.4 us -> 64.2 us (1.013)
  the two profiles are of different devices: /device:TPU:69 before, /device:TPU:1 now
where the time goes in v7:
time: 64.2 us; the launch traced here: 64 us
  Pallas kernels  61.4 us (96%)
  local copies, waits for them, and re-layouts  1.98 us (3%)
    pallas_call x1, Pallas kernels, on_device(): pl.pallas_call(kernel, out_shape=(V((CELLS, 2, CH), BF), V((CELLS, 2, CH)...  61.4 us
    unnamed x3, local copies, waits for them, and re-layouts  1.98 us

profile of v7, /device:TPU:1, one launch (start us, length us, event | category | flops | bytes accessed | tf_op | source)
XLA Modules:
  0.0 64.0 jit_solution(12793313576182150869)
XLA Ops:
  0.6 61.4 %block.1 = (bf16[196,2,256]{2,1,0:T(2,128)(2,1)S(1)}, bf16[196,2,256]{2,1,0:T(2,128)(2,1)S(1)}, f32[48,256]{1,0:T(8,128)S(1)}) custom-call(bf16[196,2,256]{2,1,0:T(2,128)(2,1)} %bitcast.16, bf16[3,3,64,256]{3,2,1,0:T(8,128)(2,1)} %cw_h.1, bf16[256,1024]{1,0:T(8,128)(2,1)} %down_h.1, bf16[1024,256]{1,0:T(8,128)(2,1)} %up_h.1, bf16[256,3072]{1,0:T(8,128)(2,1)} %w_h.1, ...), custom_call_target="tpu_custom_call" | custom-call | tf_op jit(solution)/shard_map/block/pallas_call | solution.py:477
  62.0 0.7 %copy.12 = bf16[2,14,14,256]{3,0,2,1:T(2,128)(2,1)} copy(bf16[2,14,14,256]{3,0,2,1:T(2,128)(2,1)S(1)} %bitcast.14) | data formatting | bytes 401408
  62.7 0.7 %copy.13 = bf16[2,14,14,256]{3,0,2,1:T(2,128)(2,1)} copy(bf16[2,14,14,256]{3,0,2,1:T(2,128)(2,1)S(1)} %bitcast.13) | data formatting | bytes 401408
  63.4 0.6 copy.14

commit v8 on v5

--- a/solution.py
+++ b/solution.py
@@ -394,7 +394,6 @@
         p_copies.append(go(rcopy(
             psend.at[(zl + k) % NZL], precv.at[k - 1], dev(zl_=(zl + k) % NZL))))
 
-    y_second(0)
     for d in (1, -1):
         a, n = HALF[d]
         q_rel[d].wait_recv()
@@ -402,10 +401,8 @@
         q_comb[d] = go(rcopy(
             qcs.at[pl.ds(a, n), :], qcomb.at[pl.ds(a, n), :], dev(x_=xp[d])))
 
-    for j in range(1, 4):
+    for j in range(4):
         y_second(j)
-    z_push(0)
-    z_push(1)
 
     for d in (1, -1):
         q_dir[d].wait_recv()
@@ -415,8 +412,8 @@
     pre_grad = gate_grad * gating * (1.0 - gating)
     se2[ch] = join3(dot_nt(split3(pre_grad), up_v[...]))
     se_copies = se_push(se2)
-    z_push(2)
-    z_push(3)
+    for j in range(4):
+        z_push(j)
 
     for c in p_copies:
         c.wait_recv()

time: 63.4 us -> 64 us (level)
  the two profiles are of different devices: /device:TPU:69 before, /device:TPU:5 now
where the time goes in v8:
time: 64 us; the launch traced here: 63.8 us
  Pallas kernels  61 us (95%)
  local copies, waits for them, and re-layouts  2.14 us (3%)
  between operations  0.64 us (1%)
    pallas_call x1, Pallas kernels, on_device(): pl.pallas_call(kernel, out_shape=(V((VALID, CH), BF), V((VALID, CH), BF),...  61 us
    reshape x2, local copies, waits for them, and re-layouts, images_of(): return jnp.transpose(v.reshape(14, 14, 2, CH), (2, 0, 1, 3))  1.52 us

profile of v8, /device:TPU:5, one launch (start us, length us, event | category | flops | bytes accessed | tf_op | source)
XLA Modules:
  0.0 63.8 jit_solution(11016493688293623675)
XLA Ops:
  0.6 61.0 %block.1 = (bf16[392,256]{1,0:T(8,128)(2,1)S(1)}, bf16[392,256]{1,0:T(8,128)(2,1)S(1)}, f32[48,256]{1,0:T(8,128)S(1)}) custom-call(bf16[196,2,256]{2,1,0:T(2,128)(2,1)} %bitcast.10, bf16[3,3,64,256]{3,2,1,0:T(8,128)(2,1)} %cw_h.1, bf16[256,1024]{1,0:T(8,128)(2,1)} %down_h.1, bf16[1024,256]{1,0:T(8,128)(2,1)} %up_h.1, bf16[256,3072]{1,0:T(8,128)(2,1)} %w_h.1, ...), custom_call_target="tpu_custom_call" | custom-call | tf_op jit(solution)/shard_map/block/pallas_call | solution.py:470
  61.7 0.8 %reshape.20 = bf16[14,14,2,256]{3,2,1,0:T(2,128)(2,1)} reshape(bf16[392,256]{1,0:T(8,128)(2,1)S(1)} %get-tuple-element.6) | data formatting | bytes 401408 | tf_op jit(solution)/shard_map/reshape | solution.py:465
  62.4 0.6 copy.10
  63.1 0.8 %reshape.21 = bf16[14,14,2,256]{3,2,1,0:T(2,128)(2,1)} reshape(bf16[392,256]{1,0:T(8,128)(2,1)S(1)} %get-tuple-element.7) | data formatting | bytes 401408 | tf_op jit(solution)/shard_map/reshape | solution.py:465
